TPU v7x, 128 devices: a whole 4x4x4 slice. The times are simulated.
128 devices in a mesh: dp: 8 (over x, y_lo), tensor: 16 (over y_hi, z, core).
Axes of the slice: x: 4, y: 4 (y_hi: 2, y_lo: 2; y = y_hi * 2 + y_lo), z: 4, core: 2. Of those that a mesh axis runs over, the one named last changes fastest.
Arguments:
- enc_tokens: bfloat16 [128, 128, 1024], P(('dp', 'tensor')), may hold values from -6 to 6
- src_lengths: int32 [128], replicated, may hold values from 1 to 128, as said below
- enc_gain: float32 [1024], replicated, may hold values from 0.1 to 1.9
- enc_query: bfloat16 [1024, 8192], P(None, 'tensor'), may hold values from -0.1875 to 0.1875
- enc_key: bfloat16 [1024, 8192], P(None, 'tensor'), may hold values from -0.1875 to 0.1875
- enc_value: bfloat16 [1024, 8192], P(None, 'tensor'), may hold values from -0.1875 to 0.1875
- enc_output: bfloat16 [8192, 1024], P('tensor'), may hold values from -0.0625 to 0.0625
- enc_bias: float32 [64, 33], P('tensor'), may hold values from -3 to 260
- mem_gain: float32 [1024], replicated, may hold values from 0.1 to 1.9
- dec_tokens: bfloat16 [128, 64, 1024], P(('dp', 'tensor')), may hold values from -6 to 6
- tgt_lengths: int32 [128], P(('dp', 'tensor')), may hold values from 1 to 64
- lang_tags: int32 [128], P('dp'), may hold values from 0 to 7
- lang_table: bfloat16 [8, 1024], replicated, may hold values from -6 to 6
- cross_gain: float32 [1024], replicated, may hold values from 0.1 to 1.9
- cross_query: bfloat16 [1024, 8192], P(None, 'tensor'), may hold values from -0.1875 to 0.1875
- cross_key: bfloat16 [1024, 8192], P(None, 'tensor'), may hold values from -0.1875 to 0.1875
- cross_value: bfloat16 [1024, 8192], P(None, 'tensor'), may hold values from -0.1875 to 0.1875
- cross_output: bfloat16 [8192, 1024], P('tensor'), may hold values from -0.0625 to 0.0625
- ffn_gain: float32 [1024], replicated, may hold values from 0.1 to 1.9
- ffn_in: bfloat16 [1024, 32768], P(None, 'tensor'), may hold values from -0.1875 to 0.1875
- ffn_out: bfloat16 [32768, 1024], P('tensor'), may hold values from -0.03125 to 0.03125
Outputs:
- enc_memory: bfloat16 [128, 128, 1024], P(('dp', 'tensor'))
- dec_out: bfloat16 [128, 64, 1024], P(('dp', 'tensor'))
Inputs may be any that keep to these rules, and one draw needn't show every extreme that they name: `src_lengths`: never falling along the batch; the first is 1 and the last is 128.
All inputs are finite; a program needn't handle non-finite values.
Results may differ from a plain program's by a relative error of at most 0.014.
Values may be sent and summed in bfloat16 or wider, within the bound.
A program may use at most 128 MiB of HBM per device.

v0:
```python
import jax
import jax.numpy as jnp
from jax import lax
from jax.sharding import PartitionSpec as P

HD = 128
MAXREL = 16
NB = 33


EPSILON = 1e-06
NEG_FILL = -1e30


def rms_norm(values, norm_gain):
    mean_sq = jnp.mean(values * values, axis=-1, keepdims=True)
    return values * lax.rsqrt(mean_sq + EPSILON) * norm_gain


def make_grid(bias_table, query_len, key_len):
    offset = jnp.arange(key_len)[None, :] - jnp.arange(query_len)[:, None]
    bucket = (jnp.clip(offset, -MAXREL, MAXREL) + MAXREL).reshape(1, query_len * key_len)
    onehot = (bucket == jnp.arange(NB)[:, None]).astype(jnp.float32)
    flat_grid = jnp.dot(
        bias_table, onehot, precision=lax.Precision.HIGHEST, preferred_element_type=jnp.float32
    )
    return flat_grid.reshape(bias_table.shape[0], query_len, key_len)


def attend(query_rows, key_rows, value_rows, bias_table, lengths):
    examples, query_len, columns = query_rows.shape
    key_len = key_rows.shape[1]
    head_count = columns // HD
    query_heads = query_rows.reshape(examples, query_len, head_count, HD)
    key_heads = key_rows.reshape(examples, key_len, head_count, HD)
    value_heads = value_rows.reshape(examples, key_len, head_count, HD)
    scores = jnp.einsum(
        "eqhd,ekhd->ehqk", query_heads, key_heads, preferred_element_type=jnp.float32
    )
    scores = scores * HD ** (-0.5)
    if bias_table is not None:
        scores = scores + make_grid(bias_table, query_len, key_len)[None]
    key_valid = jnp.arange(key_len)[None, :] < lengths[:, None]
    scores = jnp.where(key_valid[:, None, None, :], scores, NEG_FILL)
    row_max = jnp.max(scores, axis=-1, keepdims=True)
    exponent = jnp.exp(scores - row_max)
    weights = (exponent / jnp.sum(exponent, axis=-1, keepdims=True)).astype(jnp.bfloat16)
    context = jnp.einsum(
        "ehqk,ekhd->eqhd", weights, value_heads, preferred_element_type=jnp.float32
    )
    return context.astype(jnp.bfloat16).reshape(examples, query_len, columns)


def widen(values):
    return lax.all_gather(values, "tensor", axis=0, tiled=True)


def narrow(partial_value):
    return lax.psum_scatter(
        partial_value.astype(jnp.bfloat16), "tensor", scatter_dimension=0, tiled=True
    ).astype(jnp.float32)


def restripe(values):
    groups = lax.axis_size("dp")
    per_pair = values.shape[0] // groups
    shaped = values.reshape((per_pair, groups) + values.shape[1:])
    arrived = lax.all_to_all(shaped, "dp", split_axis=1, concat_axis=0, tiled=True)
    return arrived.reshape(values.shape)


def project(rows, weight):
    flat_rows = rows.reshape(-1, rows.shape[-1])
    result = jnp.dot(flat_rows, weight, preferred_element_type=jnp.float32).astype(jnp.bfloat16)
    return result.reshape(rows.shape[:-1] + (weight.shape[1],))


def output_terms(context, weight):
    flat_rows = context.reshape(-1, context.shape[-1])
    result = jnp.dot(flat_rows, weight, preferred_element_type=jnp.float32)
    return result.reshape(context.shape[:-1] + (weight.shape[1],))


def on_device(
    enc_tokens,
    src_lengths,
    enc_gain,
    enc_query,
    enc_key,
    enc_value,
    enc_output,
    enc_bias,
    mem_gain,
    dec_tokens,
    tgt_lengths,
    lang_tags,
    lang_table,
    cross_gain,
    cross_query,
    cross_key,
    cross_value,
    cross_output,
    ffn_gain,
    ffn_in,
    ffn_out,
):
    groups = lax.axis_size("dp")
    group_index = lax.axis_index("dp")
    tensor_index = lax.axis_index("tensor")
    local_ex = enc_tokens.shape[0]
    examples = local_ex * lax.axis_size("tensor")
    per_pair = examples // groups
    enc_len = lax.dynamic_slice_in_dim(src_lengths, group_index * examples, examples)
    dec_src_len = lax.dynamic_index_in_dim(
        src_lengths.reshape(groups, per_pair, groups), group_index, axis=2, keepdims=False
    ).reshape(examples)
    enc_input = enc_tokens.astype(jnp.float32)
    enc_normed = rms_norm(enc_input, enc_gain).astype(jnp.bfloat16)
    enc_rows = widen(enc_normed)
    enc_context = attend(
        project(enc_rows, enc_query),
        project(enc_rows, enc_key),
        project(enc_rows, enc_value),
        enc_bias,
        enc_len,
    )
    enc_hidden = enc_input + narrow(output_terms(enc_context, enc_output))
    enc_memory = rms_norm(enc_hidden, mem_gain).astype(jnp.bfloat16)
    dec_memory = restripe(widen(enc_memory))
    cross_k = project(dec_memory, cross_key)
    cross_v = project(dec_memory, cross_value)
    lang_onehot = (lang_tags[:, None] == jnp.arange(lang_table.shape[0])[None, :]).astype(
        jnp.bfloat16
    )
    lang_rows = jnp.dot(lang_onehot, lang_table, preferred_element_type=jnp.float32)[:, None, :]
    dec_full = widen(dec_tokens).astype(jnp.float32) + lang_rows
    dec_normed = rms_norm(dec_full, cross_gain).astype(jnp.bfloat16)
    cross_context = attend(project(dec_normed, cross_query), cross_k, cross_v, None, dec_src_len)
    cross_terms = output_terms(cross_context, cross_output)
    local_lang = lax.dynamic_slice_in_dim(lang_rows, tensor_index * local_ex, local_ex, 0)
    hidden_local = dec_tokens.astype(jnp.float32) + local_lang + narrow(cross_terms)
    ffn_rows = widen(rms_norm(hidden_local, ffn_gain).astype(jnp.bfloat16))
    flat_rows = ffn_rows.reshape(-1, ffn_rows.shape[-1])
    activated = jnp.maximum(
        jnp.dot(flat_rows, ffn_in, preferred_element_type=jnp.float32), 0.0
    ).astype(jnp.bfloat16)
    activated = activated.reshape(ffn_rows.shape[:-1] + (ffn_in.shape[1],))
    dec_sum = hidden_local + narrow(output_terms(activated, ffn_out))
    target_len = dec_tokens.shape[1]
    keep = jnp.arange(target_len)[None, :] < tgt_lengths[:, None]
    dec_out = jnp.where(keep[:, :, None], dec_sum, 0.0).astype(jnp.bfloat16)
    return (enc_memory, dec_out)


def solution(mesh):
    in_specs = (
        P(("dp", "tensor"), None, None),
        P(),
        P(),
        P(None, "tensor"),
        P(None, "tensor"),
        P(None, "tensor"),
        P("tensor", None),
        P("tensor", None),
        P(),
        P(("dp", "tensor"), None, None),
        P(("dp", "tensor")),
        P("dp"),
        P(),
        P(),
        P(None, "tensor"),
        P(None, "tensor"),
        P(None, "tensor"),
        P("tensor", None),
        P(),
        P(None, "tensor"),
        P("tensor", None),
    )
    out_specs = (P(("dp", "tensor"), None, None), P(("dp", "tensor"), None, None))
    return jax.shard_map(
        on_device, mesh=mesh, in_specs=in_specs, out_specs=out_specs, check_vma=False
    )
```

profile of v0, /device:TPU:0, one launch (start us, length us, event | category | flops | bytes accessed | tf_op | source)
XLA Modules:
  0.0 565.8 jit_solution(7086477349250466452)
XLA Ops:
  12.4 56.7 %all-gather.5.cloned.1.call-done = bf16[16,128,1024]{2,1,0:T(8,128)(2,1)} async-done(((bf16[1,128,1024]{2,1,0:T(8,128)(2,1)}), bf16[16,128,1024]{2,1,0:T(8,128)(2,1)}) %all-gather.5.cloned.1.call-update) | async-done | bytes 4194320 | tf_op jit(solution)/shard_map/all_gather | solution.py:55
  69.0 5.9 %convolution_convert_fusion.2 = bf16[2048,512]{1,0:T(8,128)(2,1)} fusion(bf16[2048,1024]{1,0:T(8,128)(2,1)} %bitcast.61, bf16[1024,512]{1,0:T(8,128)(2,1)S(1)} %copy-done.16), kind=kOutput, calls=%fused_computation.11 | convolution fusion | flops 2148532224 | bytes 7340032 | tf_op jit(solution)/shard_map/dot_general | solution.py:74
  74.9 2.5 reshape_reshape.26
  77.5 6.3 %convolution_convert_fusion.3 = bf16[2048,512]{1,0:T(8,128)(2,1)} fusion(bf16[2048,1024]{1,0:T(8,128)(2,1)} %bitcast.62, bf16[1024,512]{1,0:T(8,128)(2,1)} %param.24), kind=kOutput, calls=%fused_computation.12 | convolution fusion | flops 2148532224 | bytes 7340032 | tf_op jit(solution)/shard_map/dot_general | solution.py:74
  83.8 3.7 convolution_convert_fusion.4
  87.5 4.0 reshape_reshape.24
  91.4 4.0 reshape_reshape.25
  95.4 3.2 fusion.10
  101.3 4.3 convolution_convert_fusion.5
  105.7 78.5 %reduce-scatter.4.cloned.1.call-done = bf16[1,128,1024]{2,1,0:T(8,128)(2,1)} async-done(((bf16[16,128,1024]{2,1,0:T(8,128)(2,1)}), bf16[1,128,1024]{2,1,0:T(8,128)(2,1)}) %reduce-scatter.4.cloned.1.call-update) | async-done | bytes 262160 | tf_op jit(solution)/shard_map/reduce_scatter | solution.py:59
  187.7 54.1 %all-gather.7.cloned.1.call-done = bf16[16,128,1024]{2,1,0:T(8,128)(2,1)} async-done(((bf16[1,128,1024]{2,1,0:T(8,128)(2,1)}), bf16[16,128,1024]{2,1,0:T(8,128)(2,1)}) %all-gather.7.cloned.1.call-update) | async-done | bytes 4194320 | tf_op jit(solution)/shard_map/all_gather | solution.py:55
  241.8 4.8 copy.70
  246.6 4.7 all-to-all-start
  252.3 60.9 %all-gather.9.cloned.1.call-done = bf16[16,64,1024]{2,1,0:T(8,128)(2,1)} async-done(((bf16[1,64,1024]{2,1,0:T(8,128)(2,1)}), bf16[16,64,1024]{2,1,0:T(8,128)(2,1)}) %all-gather.9.cloned.1.call-update) | async-done | bytes 2097168 | tf_op jit(solution)/shard_map/all_gather | solution.py:55
  313.2 2.4 multiply_reduce_fusion
  319.3 5.9 %convolution_convert_fusion = bf16[2048,512]{1,0:T(8,128)(2,1)} fusion(bf16[2048,1024]{1,0:T(8,128)(2,1)} %bitcast.11, bf16[1024,512]{1,0:T(8,128)(2,1)S(1)} %copy-done.19), kind=kOutput, calls=%fused_computation.9 | convolution fusion | flops 2148532224 | bytes 7340032 | tf_op jit(solution)/shard_map/dot_general | solution.py:74
  325.3 4.5 convolution_convert_fusion.1
  331.9 2.5 reshape_reshape.30
  338.9 9.8 %fusion.25 = bf16[16,4,8,8,128]{4,3,2,1,0:T(8,128)(2,1)} fusion(bf16[16,128,4,128]{3,2,1,0:T(4,128)(2,1)S(1)} %copy-done.6, f32[16,4,64]{2,1,0:T(4,128)S(1)} %fusion.55, f32[16,4,64,128]{3,2,1,0:T(8,128)} %copy-done.7, pred[16,128]{1,0:T(8,128)(4,1)S(1)} %iota_compare_fusion.4), kind=kOutput, calls=%fused_computation.41 | convolution fusion | flops 137367680 | bytes 5261312 | tf_op jit(solution)/shard_map/ehqk,ekhd->eqhd/dot_general | solution.py:48
  348.7 3.8 convolution_convert_fusion.7
  352.7 70.8 %reduce-scatter.6.cloned.1.call-done = bf16[1,64,1024]{2,1,0:T(8,128)(2,1)} async-done(((bf16[16,64,1024]{2,1,0:T(8,128)(2,1)}), bf16[1,64,1024]{2,1,0:T(8,128)(2,1)}) %reduce-scatter.6.cloned.1.call-update) | async-done | bytes 131088 | tf_op jit(solution)/shard_map/reduce_scatter | solution.py:59
  426.6 46.4 %all-gather.11.cloned.1.call-done = bf16[16,64,1024]{2,1,0:T(8,128)(2,1)} async-done(((bf16[1,64,1024]{2,1,0:T(8,128)(2,1)}), bf16[16,64,1024]{2,1,0:T(8,128)(2,1)}) %all-gather.11.cloned.1.call-update) | async-done | bytes 2097168 | tf_op jit(solution)/shard_map/all_gather | solution.py:55
  473.0 14.3 %convolution_convert_fusion.6 = bf16[1024,1024]{1,0:T(8,128)(2,1)} fusion(bf16[2048,1024]{1,0:T(8,128)(2,1)} %param.41, bf16[1024,1024]{1,0:T(8,128)(2,1)} %bitcast.64, bf16[1024,2048]{1,0:T(8,128)(2,1)} %param.40), kind=kOutput, calls=%fused_computation.36 | convolution fusion | flops 8595177472 | bytes 12582912 | tf_op jit(solution)/shard_map/dot_general | solution.py:80
  488.0 69.2 %reduce-scatter.8.cloned.1.call-done = bf16[1,64,1024]{2,1,0:T(8,128)(2,1)} async-done(((bf16[16,64,1024]{2,1,0:T(8,128)(2,1)}), bf16[1,64,1024]{2,1,0:T(8,128)(2,1)}) %reduce-scatter.8.cloned.1.call-update) | async-done | bytes 131088 | tf_op jit(solution)/shard_map/reduce_scatter | solution.py:59
  (91 shorter events, 27.4 us)
Async XLA Ops:
  7.2 94.2 %copy-start = (bf16[512,1024]{1,0:T(8,128)(2,1)S(1)}, bf16[512,1024]{1,0:T(8,128)(2,1)}, u32[]{:S(2)}) copy-start(bf16[512,1024]{1,0:T(8,128)(2,1)} %param.27) | copy-start | bytes 3145732
  7.2 5.0 copy-start.14
  7.2 61.8 %copy-start.16 = (bf16[1024,512]{1,0:T(8,128)(2,1)S(1)}, bf16[1024,512]{1,0:T(8,128)(2,1)}, u32[]{:S(2)}) copy-start(bf16[1024,512]{1,0:T(8,128)(2,1)} %param.25) | copy-start | bytes 3145732
  7.2 61.8 %all-gather.5.cloned.1.call-start = ((), (), s32[]{:S(2)}) async-start(), calls=%async_computation.4 | async-start | bytes 4456448 | tf_op jit(solution)/shard_map/all_gather | solution.py:55
  10.3 173.9 %reduce-scatter.4.cloned.1.call-start = ((), (), s32[]{:S(2)}) async-start(), calls=%async_computation.5 | async-start | bytes 4456448 | tf_op jit(solution)/shard_map/reduce_scatter | solution.py:59
  77.4 6.3 %copy-start.15 = (bf16[16,128,1024]{2,1,0:T(8,128)(2,1)S(1)}, bf16[16,128,1024]{2,1,0:T(8,128)(2,1)}, u32[]{:S(2)}) copy-start(bf16[16,128,1024]{2,1,0:T(8,128)(2,1)} %all-gather.5.cloned.1.call-done) | copy-start | bytes 12582916
  77.4 6.3 %copy-start.17 = (bf16[1024,512]{1,0:T(8,128)(2,1)S(1)}, bf16[1024,512]{1,0:T(8,128)(2,1)}, u32[]{:S(2)}) copy-start(bf16[1024,512]{1,0:T(8,128)(2,1)} %param.26) | copy-start | bytes 3145732
  105.7 78.6 %copy-start.3 = (bf16[1,128,1024]{2,1,0:T(8,128)(2,1)S(1)}, bf16[1,128,1024]{2,1,0:T(8,128)(2,1)}, u32[]{:S(2)}) copy-start(bf16[1,128,1024]{2,1,0:T(8,128)(2,1)} %param.21) | copy-start | bytes 786436
  105.7 79.7 %copy-start.10 = (f32[1024]{0:T(1024)S(1)}, f32[1024]{0:T(1024)}, u32[]{:S(2)}) copy-start(f32[1024]{0:T(1024)} %param.29) | copy-start | bytes 12292
  105.7 136.1 %all-gather.7.cloned.1.call-start = ((), (), s32[]{:S(2)}) async-start(), calls=%async_computation.6 | async-start | bytes 4456448 | tf_op jit(solution)/shard_map/all_gather | solution.py:55
  187.2 126.1 %all-gather.9.cloned.1.call-start = ((), (), s32[]{:S(2)}) async-start(), calls=%async_computation.7 | async-start | bytes 2228224 | tf_op jit(solution)/shard_map/all_gather | solution.py:55
  246.6 5.5 copy-start.9
  246.6 5.5 copy-start.13
  246.6 71.8 %all-to-all-start = ((bf16[2,8,128,1024]{3,2,0,1:T(8,128)(2,1)}), bf16[2,8,128,1024]{3,2,0,1:T(8,128)(2,1)}, u32[]{:S(2)}, u32[]{:S(2)}) async-start(bf16[2,8,128,1024]{3,2,0,1:T(8,128)(2,1)} %copy.70), calls=%async_computation.1 | async-start | bytes 8388608 | tf_op jit(solution)/shard_map/all_to_all | solution.py:68
  251.3 64.3 %copy-start.11 = (f32[1024]{0:T(1024)S(1)}, f32[1024]{0:T(1024)}, u32[]{:S(2)}) copy-start(f32[1024]{0:T(1024)} %param.34) | copy-start | bytes 12292
  251.3 172.2 %reduce-scatter.6.cloned.1.call-start = ((), (), s32[]{:S(2)}) async-start(), calls=%async_computation.8 | async-start | bytes 2228224 | tf_op jit(solution)/shard_map/reduce_scatter | solution.py:59
  319.3 5.9 %copy-start.20 = (bf16[1024,512]{1,0:T(8,128)(2,1)S(1)}, bf16[1024,512]{1,0:T(8,128)(2,1)}, u32[]{:S(2)}) copy-start(bf16[1024,512]{1,0:T(8,128)(2,1)} %param.37) | copy-start | bytes 3145732
  338.9 9.8 %copy-start.21 = (bf16[512,1024]{1,0:T(8,128)(2,1)S(1)}, bf16[512,1024]{1,0:T(8,128)(2,1)}, u32[]{:S(2)}) copy-start(bf16[512,1024]{1,0:T(8,128)(2,1)} %param.38) | copy-start | bytes 3145732
  352.6 71.0 %copy-start.4 = (bf16[1,64,1024]{2,1,0:T(8,128)(2,1)S(1)}, bf16[1,64,1024]{2,1,0:T(8,128)(2,1)}, u32[]{:S(2)}) copy-start(bf16[1,64,1024]{2,1,0:T(8,128)(2,1)} %param.30) | copy-start | bytes 393220
  352.6 72.0 %copy-start.12 = (f32[1024]{0:T(1024)S(1)}, f32[1024]{0:T(1024)}, u32[]{:S(2)}) copy-start(f32[1024]{0:T(1024)} %param.39) | copy-start | bytes 12292
  352.6 120.4 %all-gather.11.cloned.1.call-start = ((), (), s32[]{:S(2)}) async-start(), calls=%async_computation.9 | async-start | bytes 2228224 | tf_op jit(solution)/shard_map/all_gather | solution.py:55
  426.3 131.0 %reduce-scatter.8.cloned.1.call-start = ((), (), s32[]{:S(2)}) async-start(), calls=%async_computation.10 | async-start | bytes 2228224 | tf_op jit(solution)/shard_map/reduce_scatter | solution.py:59
  473.0 85.9 %copy-start.1 = (bf16[512,1024]{1,0:T(8,128)(2,1)S(1)}, bf16[512,1024]{1,0:T(8,128)(2,1)}, u32[]{:S(2)}) copy-start(bf16[512,1024]{1,0:T(8,128)(2,1)} %param.27) | copy-start | bytes 3145732
  487.3 70.0 %copy-start.8 = (bf16[1,64,1024]{2,1,0:T(8,128)(2,1)S(1)}, bf16[1,64,1024]{2,1,0:T(8,128)(2,1)}, u32[]{:S(2)}) copy-start(bf16[1,64,1024]{2,1,0:T(8,128)(2,1)} %reduce-scatter.6.cloned.1.call-done) | copy-start | bytes 393220
  (6 other events, 9.6 us)
Sparse Core Ops, SparseCore 0:
  11.1 57.8 all-gather.4
  105.8 78.3 reduce-scatter.3
  187.6 54.2 all-gather.6
  244.5 68.7 all-gather.8
  352.7 70.7 reduce-scatter.5
  426.4 46.5 all-gather.10
  487.5 69.7 reduce-scatter.7
where the time goes:
time: 567 us; the launch traced here: 566 us
  waiting for transfers between devices  437 us (77%)
  matrix products  67.4 us (12%)
  local copies, waits for them, and re-layouts  24.1 us (4%)
  other arithmetic  16.5 us (3%)
  between operations  15.1 us (3%)
    reduce_scatter x3, waiting for transfers between devices, narrow(): lax.psum_scatter(partial_value.astype(jnp.bfloat16), 'tensor', scatter_di...  219 us
    all_gather x4, waiting for transfers between devices, widen(): return lax.all_gather(values, 'tensor', axis=0, tiled=True)  218 us
    dot_general x6, matrix products, project(): jnp.dot(flat_rows, weight, preferred_element_type=jnp.float32)  27.6 us
    dot_general x3, matrix products, output_terms(): result = jnp.dot(flat_rows, weight, preferred_element_type=jnp.float32)  22.5 us
  transfers between devices with their start and end apart: 8, of which 7 were waited for; matrix products, arithmetic and copies ran while one was open for 2% of the time, Pallas kernels for 0%

commit v1 on v0

v1 whole, which is shorter than its diff:
```python
import functools

import jax
import jax.numpy as jnp
from jax import lax
from jax.experimental import pallas as pl
from jax.experimental.pallas import tpu as pltpu
from jax.sharding import PartitionSpec as P

D = 1024
HD = 128
SRC = 128
TGT = 64
MAXREL = 16
NB = 33
LANGS = 8
HEADS = 4
HW = HEADS * HD
FF = 2048
EPSILON = 1e-06
NEG_FILL = -1e30
SCALE = HD ** (-0.5)
MESH = pl.DeviceIdType.MESH
F32 = jnp.float32
BF16 = jnp.bfloat16

ORDER = ((0, 0), (0, 1), (0, 3), (1, 0), (0, 2), (1, 1), (1, 3), (1, 2))
DY_BITS = sum(dy << i for i, (dy, dz) in enumerate(ORDER))
DZ_BITS = sum(dz << (2 * i) for i, (dy, dz) in enumerate(ORDER))


def rms(values, gain):
    mean_sq = jnp.mean(values * values, axis=-1, keepdims=True)
    return values * lax.rsqrt(mean_sq + EPSILON) * gain


class Place:
    def __init__(self):
        self.me = lax.axis_index("tensor")
        self.dp = lax.axis_index("dp")
        self.core = self.me % 2
        self.z = (self.me // 2) % 4
        self.y = self.me // 8

    def chip(self, dy, dz):
        return ((self.y + dy) % 2) * 4 + (self.z + dz) % 4

    def slot(self, dy, dz, dk=0):
        return self.chip(dy, dz) * 2 + (self.core + dk) % 2

    def near(self):
        return (self.slot(0, 0, 1), self.slot(0, 1), self.slot(0, 3), self.slot(1, 0))


def send(src, dst, send_sem, recv_sem, device):
    pltpu.make_async_remote_copy(
        src_ref=src,
        dst_ref=dst,
        send_sem=send_sem,
        recv_sem=recv_sem,
        device_id=device,
        device_id_type=MESH,
    ).start()


def arrived(dst, recv_sem):
    pltpu.make_async_copy(dst, dst, recv_sem).wait()


class Gather:
    def __init__(self, place, buf, ssem, rsem, hsem):
        self.p, self.buf = place, buf
        self.ssem, self.rsem, self.hsem = ssem, rsem, hsem
        self.half = buf.shape[1] // 2
        self.sent = []

    def _send(self, src, recv_sem, target):
        sem = self.ssem.at[len(self.sent)]
        send(src, src, sem, recv_sem, {"tensor": target})
        self.sent.append(src.shape[0])

    def _full(self, slot, target):
        self._send(self.buf.at[slot], self.rsem.at[slot], target)

    def _half(self, slot, dy, which, target):
        part = self.buf.at[slot, pl.ds(which * self.half, self.half)]
        self._send(part, self.hsem.at[dy, which], target)

    def start(self):
        p = self.p
        for target in (p.slot(0, 1), p.slot(0, 3), p.slot(1, 0), p.slot(0, 0, 1)):
            self._full(p.me, target)

    def event(self, index):
        p = self.p
        dy, dz = ORDER[index]
        slot = p.slot(dy, dz)
        partner = p.slot(0, 0, 1)
        if dz == 2:
            for which in (0, 1):
                arrived(
                    self.buf.at[slot, pl.ds(which * self.half, self.half)], self.hsem.at[dy, which]
                )
        else:
            arrived(self.buf.at[slot], self.rsem.at[slot])
        if dz == 1:
            self._half(slot, dy, 1, p.slot(0, 3))
        elif dz == 3:
            self._half(slot, dy, 0, p.slot(0, 1))
        elif dz == 0:
            self._full(slot, p.slot(0, 1))
            self._full(slot, p.slot(0, 3))
        self._full(slot, partner)

    def partner_wait(self, chip):
        slot = chip * 2 + (self.p.core + 1) % 2
        arrived(self.buf.at[slot], self.rsem.at[slot])

    def drain(self):
        for index, rows in enumerate(self.sent):
            arrived(self.buf.at[0, pl.ds(0, rows)], self.ssem.at[index])


GATHER_SENDS = 17


def order_chip(place, index):
    dy = (DY_BITS >> index) & 1
    dz = (DZ_BITS >> (2 * index)) & 3
    return place.chip(dy, dz)


def scatter_chip(place, index):
    return place.chip(1 - index // 4, (2 - index % 4) % 4)


class Scatter:
    def __init__(self, place, part, xbuf, relay, fin, yrec, ysend, psem, xsem, ssem, zsem, fsem, ysem):
        self.p, self.part, self.xbuf, self.relay = place, part, xbuf, relay
        self.fin, self.yrec, self.ysend = fin, yrec, ysend
        self.psem, self.xsem, self.ssem = psem, xsem, ssem
        self.zsem, self.fsem, self.ysem = zsem, fsem, ysem
        self.half = part.shape[1] // 2
        self.sent = []

    def partner_send(self, chip):
        slot = chip * 2 + (self.p.core + 1) % 2
        send(
            self.part.at[slot],
            self.xbuf.at[chip],
            self.psem.at[chip],
            self.xsem.at[chip],
            {"tensor": self.p.slot(0, 0, 1)},
        )

    def partner_add(self, chip):
        arrived(self.xbuf.at[chip], self.xsem.at[chip])
        slot = chip * 2 + self.p.core
        self.part[slot] = self.part[slot] + self.xbuf[chip]

    def _send(self, src, dst, recv_sem, target):
        sem = self.ssem.at[len(self.sent)]
        send(src, dst, sem, recv_sem, {"tensor": target})
        self.sent.append(src.shape[0])

    def _rows(self, which):
        return pl.ds(which * self.half, self.half)

    def far(self, dy):
        p = self.p
        slot = p.slot(dy, 2)
        for which, dz in ((0, 1), (1, 3)):
            self._send(
                self.part.at[slot, self._rows(which)],
                self.relay.at[dy, which],
                self.zsem.at[dy, which],
                p.slot(0, dz),
            )

    def near_half(self, dy, way, which):
        p = self.p
        dz = (1, 3)[way]
        rows = self._rows(which)
        self._send(
            self.part.at[p.slot(dy, dz), rows],
            self.fin.at[dy, way, rows],
            self.fsem.at[dy, way, which],
            p.slot(0, dz),
        )

    def relay_add(self, dy, way):
        p = self.p
        arrived(self.relay.at[dy, way], self.zsem.at[dy, way])
        slot, rows = p.slot(dy, (1, 3)[way]), self._rows(way)
        self.part[slot, rows, :] = self.part[slot, rows, :] + self.relay[dy, way]

    def ring_sum(self, dy):
        for way in (0, 1):
            for which in (0, 1):
                arrived(self.fin.at[dy, way, self._rows(which)], self.fsem.at[dy, way, which])
        slot = self.p.slot(dy, 0)
        return (
            self.part[slot].astype(F32) + self.fin[dy, 0].astype(F32) + self.fin[dy, 1].astype(F32)
        )

    def finish(self):
        p = self.p
        for dy in (1, 0):
            self.far(dy)
            self.near_half(dy, 0, 1)
            self.near_half(dy, 1, 0)
        for dy in (1, 0):
            for way in (0, 1):
                self.relay_add(dy, way)
            for way in (0, 1):
                self.near_half(dy, way, way)
        self.ysend[...] = self.ring_sum(1).astype(BF16)
        own = self.ring_sum(0)
        self._send(self.ysend, self.yrec, self.ysem, p.slot(1, 0))
        arrived(self.yrec, self.ysem)
        return own + self.yrec[...].astype(F32)

    def drain(self):
        for chip in range(8):
            slot = chip * 2 + (self.p.core + 1) % 2
            arrived(self.part.at[slot], self.psem.at[chip])
        for index, rows in enumerate(self.sent):
            arrived(self.part.at[0, pl.ds(0, rows)], self.ssem.at[index])


def gather_scratch(rows):
    return [
        pltpu.VMEM((16, rows, D), BF16),
        pltpu.SemaphoreType.DMA((GATHER_SENDS,)),
        pltpu.SemaphoreType.DMA((16,)),
        pltpu.SemaphoreType.DMA((2, 2)),
    ]


def scatter_scratch(rows):
    return [
        pltpu.VMEM((16, rows, D), BF16),
        pltpu.VMEM((8, rows, D), BF16),
        pltpu.VMEM((2, 2, rows // 2, D), BF16),
        pltpu.VMEM((2, 2, rows, D), BF16),
        pltpu.VMEM((rows, D), BF16),
        pltpu.VMEM((rows, D), BF16),
        pltpu.SemaphoreType.DMA((8,)),
        pltpu.SemaphoreType.DMA((8,)),
        pltpu.SemaphoreType.DMA((13,)),
        pltpu.SemaphoreType.DMA((2, 2)),
        pltpu.SemaphoreType.DMA((2, 2, 2)),
        pltpu.SemaphoreType.DMA,
    ]


GATHER_N = 4
SCATTER_N = 12


def greet(devices):
    barrier = pltpu.get_barrier_semaphore()
    for device in devices:
        pl.semaphore_signal(barrier, inc=1, device_id=device, device_id_type=MESH)
    return barrier


def dot(left, right):
    return jnp.dot(left, right, preferred_element_type=F32)


def softmax_weights(scores):
    row_max = jnp.max(scores, axis=-1, keepdims=True)
    exponent = jnp.exp(scores - row_max)
    return (exponent * (1.0 / jnp.sum(exponent, axis=-1, keepdims=True))).astype(BF16)


def dot_t(left, right):
    return lax.dot_general(left, right, (((1,), (1,)), ((), ())), preferred_element_type=F32)


def enc_kernel(
    tokens, lengths, gain, wq_h, wk_h, wv_h, wo_h, bias, mem_gain, out, wq, wk, wv, wo, grid, ctx, wsem, *rest
):
    place = Place()
    gather = Gather(place, *rest[:GATHER_N])
    scatter = Scatter(place, *rest[GATHER_N:])
    buf, part = rest[0], rest[GATHER_N]
    loads = [
        pltpu.make_async_copy(src, dst, wsem.at[i])
        for i, (src, dst) in enumerate(((wq_h, wq), (wk_h, wk), (wv_h, wv), (wo_h, wo)))
    ]
    buf[place.me] = rms(tokens[0].astype(F32), gain[...]).astype(BF16)
    barrier = greet([{"tensor": t} for t in place.near()])
    for load in loads:
        load.start()
    pl.semaphore_wait(barrier, 4)
    gather.start()

    keys = lax.broadcasted_iota(jnp.int32, (SRC, SRC), 1)
    bucket = jnp.clip(keys - lax.broadcasted_iota(jnp.int32, (SRC, SRC), 0), -MAXREL, MAXREL) + MAXREL
    for head in range(HEADS):
        values = jnp.zeros((SRC, SRC), F32)
        for index in range(NB):
            values = jnp.where(bucket == index, bias[head, index], values)
        grid[head] = values
    for load in loads:
        load.wait()

    def step(index, carry):
        @pl.when(index == 1)
        def _():
            for event in (1, 2, 3):
                gather.event(event)

        @pl.when(index == 4)
        def _():
            for event in (4, 5, 6):
                gather.event(event)

        @pl.when(index == 7)
        def _():
            gather.event(7)

        chip = order_chip(place, index)
        gather.partner_wait(chip)
        rows = buf[pl.ds(chip * 2, 2)].reshape(2 * SRC, D)
        columns = lax.broadcasted_iota(jnp.int32, (SRC, SRC), 1)
        for pair in range(HEADS // 2):
            wide = slice(pair * 2 * HD, (pair + 1) * 2 * HD)
            q = dot(rows, wq[:, wide]).astype(BF16)
            k = dot(rows, wk[:, wide]).astype(BF16)
            v = dot(rows, wv[:, wide]).astype(BF16)
            for ex in range(2):
                length = lengths[place.dp * 16 + chip * 2 + ex]
                here = slice(ex * SRC, (ex + 1) * SRC)
                for head in range(2):
                    cols = slice(head * HD, (head + 1) * HD)
                    full = pair * 2 + head
                    scores = dot_t(q[here, cols], k[here, cols]) * SCALE + grid[full]
                    weights = softmax_weights(jnp.where(columns < length, scores, NEG_FILL))
                    ctx[chip * 2 + ex, :, full * HD : (full + 1) * HD] = dot(
                        weights, v[here, cols]
                    ).astype(BF16)
        return carry

    lax.fori_loop(0, 8, step, 0)

    def out_step(index, carry):
        @pl.when(index > 0)
        def _():
            scatter.partner_send(scatter_chip(place, index - 1))

        chip = scatter_chip(place, index)
        rows = ctx[pl.ds(chip * 2, 2)].reshape(2 * SRC, HW)
        part[pl.ds(chip * 2, 2)] = dot(rows, wo[...]).astype(BF16).reshape(2, SRC, D)
        return carry

    lax.fori_loop(0, 8, out_step, 0)
    scatter.partner_send(scatter_chip(place, 7))
    for index in range(8):
        scatter.partner_add(scatter_chip(place, index))
    total = tokens[0].astype(F32) + scatter.finish()
    out[0] = rms(total, mem_gain[...]).astype(BF16)
    gather.drain()
    scatter.drain()


def cross_kernel(
    memory,
    tokens,
    lengths,
    tags,
    table,
    gain,
    wq_h,
    wk_h,
    wv_h,
    wo_h,
    out,
    wq,
    wk,
    wv,
    wo,
    inp,
    q_all,
    ctx,
    wsem,
    swap_s,
    swap_r,
    *rest,
):
    place = Place()
    mem = Gather(place, *rest[:GATHER_N])
    dec = Gather(place, *rest[GATHER_N : 2 * GATHER_N])
    scatter = Scatter(place, *rest[2 * GATHER_N :])
    mem_buf, dec_buf, part = rest[0], rest[GATHER_N], rest[2 * GATHER_N]
    loads = [
        pltpu.make_async_copy(src, dst, wsem.at[i])
        for i, (src, dst) in enumerate(((wq_h, wq), (wk_h, wk), (wv_h, wv), (wo_h, wo)))
    ]
    x, y_lo = place.dp // 2, place.dp % 2
    other_dp = place.z * 2 + place.core
    other_t = place.y * 8 + x * 2 + y_lo
    stays = jnp.logical_and(other_dp == place.dp, other_t == place.me)
    moves = jnp.logical_not(stays)
    barrier = greet([{"tensor": t} for t in place.near()])

    @pl.when(moves)
    def _():
        pl.semaphore_signal(barrier, inc=1, device_id=(other_dp, other_t), device_id_type=MESH)

    tag = tags[place.me]
    lang = jnp.zeros((1, D), F32)
    for index in range(LANGS):
        lang = jnp.where(tag == index, table[index : index + 1, :].astype(F32), lang)
    value = tokens[0].astype(F32) + lang
    inp[...] = value
    dec_buf[place.me] = rms(value, gain[...]).astype(BF16)
    for load in loads:
        load.start()

    @pl.when(moves)
    def _():
        pl.semaphore_wait(barrier, 5)
        send(memory.at[0], mem_buf.at[other_t], swap_s, swap_r, (other_dp, other_t))

    @pl.when(stays)
    def _():
        pl.semaphore_wait(barrier, 4)
        pltpu.make_async_copy(memory.at[0], mem_buf.at[place.me], swap_r).start()

    dec.start()
    for event in range(1, 8):
        dec.event(event)
    for chip in range(8):
        dec.partner_wait(chip)
    arrived(mem_buf.at[place.me], swap_r)
    mem.start()
    for load in loads:
        load.wait()

    def q_step(index, carry):
        rows = dec_buf[pl.ds(index * 4, 4)].reshape(4 * TGT, D)
        q_all[pl.ds(index * 4, 4)] = dot(rows, wq[...]).astype(BF16).reshape(4, TGT, HW)
        return carry

    lax.fori_loop(0, 4, q_step, 0)

    def step(index, carry):
        @pl.when(index == 1)
        def _():
            for event in (1, 2, 3):
                mem.event(event)

        @pl.when(index == 4)
        def _():
            for event in (4, 5, 6):
                mem.event(event)

        @pl.when(index == 7)
        def _():
            mem.event(7)

        chip = order_chip(place, index)
        mem.partner_wait(chip)
        rows = mem_buf[pl.ds(chip * 2, 2)].reshape(2 * SRC, D)
        columns = lax.broadcasted_iota(jnp.int32, (TGT, SRC), 1)
        for pair in range(HEADS // 2):
            wide = slice(pair * 2 * HD, (pair + 1) * 2 * HD)
            k = dot(rows, wk[:, wide]).astype(BF16)
            v = dot(rows, wv[:, wide]).astype(BF16)
            for ex in range(2):
                row = (chip % 4) * 4 + ex * 2 + chip // 4
                length = lengths[(row // 2) * 16 + (row % 2) * 8 + place.dp]
                here = slice(ex * SRC, (ex + 1) * SRC)
                for head in range(2):
                    cols = slice(head * HD, (head + 1) * HD)
                    full = slice((pair * 2 + head) * HD, (pair * 2 + head + 1) * HD)
                    scores = dot_t(q_all[row, :, full], k[here, cols]) * SCALE
                    weights = softmax_weights(jnp.where(columns < length, scores, NEG_FILL))
                    ctx[row, :, full] = dot(weights, v[here, cols]).astype(BF16)
        return carry

    lax.fori_loop(0, 8, step, 0)

    def out_step(index, carry):
        @pl.when(index > 0)
        def _():
            scatter.partner_send(scatter_chip(place, index - 1))

        chip = scatter_chip(place, index)
        rows = ctx[pl.ds(chip * 2, 2)].reshape(2 * TGT, HW)
        part[pl.ds(chip * 2, 2)] = dot(rows, wo[...]).astype(BF16).reshape(2, TGT, D)
        return carry

    lax.fori_loop(0, 8, out_step, 0)
    scatter.partner_send(scatter_chip(place, 7))
    for index in range(8):
        scatter.partner_add(scatter_chip(place, index))
    out[...] = inp[...] + scatter.finish()

    @pl.when(moves)
    def _():
        pltpu.make_async_copy(memory.at[0], memory.at[0], swap_s).wait()

    mem.drain()
    dec.drain()
    scatter.drain()


def ffn_kernel(hidden, gain, tgt_length, win_h, wout_h, out, win, wout, act, wsem, *rest):
    place = Place()
    gather = Gather(place, *rest[:GATHER_N])
    scatter = Scatter(place, *rest[GATHER_N:])
    buf, part = rest[0], rest[GATHER_N]
    loads = [
        pltpu.make_async_copy(win_h, win, wsem.at[0]),
        pltpu.make_async_copy(wout_h, wout, wsem.at[1]),
    ]
    barrier = greet([{"tensor": t} for t in place.near()])
    for load in loads:
        load.start()
    buf[place.me] = rms(hidden[...], gain[...]).astype(BF16)
    pl.semaphore_wait(barrier, 4)
    gather.start()
    for load in loads:
        load.wait()

    def step(index, carry):
        for pair in range(4):

            @pl.when(index == pair)
            def _():
                for event in (2 * pair, 2 * pair + 1):
                    if event > 0:
                        gather.event(event)

        first, second = order_chip(place, index * 2), order_chip(place, index * 2 + 1)
        gather.partner_wait(first)
        gather.partner_wait(second)
        rows = jnp.concatenate(
            [
                buf[pl.ds(first * 2, 2)].reshape(2 * TGT, D),
                buf[pl.ds(second * 2, 2)].reshape(2 * TGT, D),
            ],
            axis=0,
        )
        for tile in range(FF // 512):
            cols = slice(tile * 512, (tile + 1) * 512)
            act[:, cols] = jnp.maximum(dot(rows, win[:, cols]), 0.0).astype(BF16)
        for tile in range(D // 256):
            cols = slice(tile * 256, (tile + 1) * 256)
            result = dot(act[...], wout[:, cols]).astype(BF16)
            part[pl.ds(first * 2, 2), :, cols] = result[: 2 * TGT].reshape(2, TGT, 256)
            part[pl.ds(second * 2, 2), :, cols] = result[2 * TGT :].reshape(2, TGT, 256)

        @pl.when(index > 0)
        def _():
            scatter.partner_send(order_chip(place, index * 2 - 2))
            scatter.partner_send(order_chip(place, index * 2 - 1))

        return carry

    lax.fori_loop(0, 4, step, 0)
    scatter.partner_send(order_chip(place, 6))
    scatter.partner_send(order_chip(place, 7))
    for index in range(8):
        scatter.partner_add(scatter_chip(place, index))
    total = hidden[...] + scatter.finish()
    keep = lax.broadcasted_iota(jnp.int32, (TGT, D), 0) < tgt_length[0]
    out[0] = jnp.where(keep, total, 0.0).astype(BF16)
    gather.drain()
    scatter.drain()


VM = pltpu.VMEM
SM = pltpu.SMEM


def call(kernel, ident, out_shape, spaces, scratch, flops, *operands):
    return pl.pallas_call(
        kernel,
        out_shape=out_shape,
        in_specs=[pl.BlockSpec(memory_space=space) for space in spaces],
        out_specs=pl.BlockSpec(memory_space=VM),
        scratch_shapes=scratch,
        compiler_params=pltpu.CompilerParams(
            collective_id=ident, has_side_effects=True, vmem_limit_bytes=58 * 2**20
        ),
        cost_estimate=pl.CostEstimate(flops=flops, bytes_accessed=8 * 2**20, transcendentals=0),
    )(*operands)


def on_device(
    enc_tokens,
    src_lengths,
    enc_gain,
    enc_query,
    enc_key,
    enc_value,
    enc_output,
    enc_bias,
    mem_gain,
    dec_tokens,
    tgt_lengths,
    lang_tags,
    lang_table,
    cross_gain,
    cross_query,
    cross_key,
    cross_value,
    cross_output,
    ffn_gain,
    ffn_in,
    ffn_out,
):
    weights = [
        pltpu.VMEM((D, HW), BF16),
        pltpu.VMEM((D, HW), BF16),
        pltpu.VMEM((D, HW), BF16),
        pltpu.VMEM((HW, D), BF16),
    ]
    enc_memory = call(
        enc_kernel,
        1,
        jax.ShapeDtypeStruct((1, SRC, D), BF16),
        (VM, SM, VM, pl.ANY, pl.ANY, pl.ANY, pl.ANY, SM, VM),
        weights
        + [
            pltpu.VMEM((HEADS, SRC, SRC), F32),
            pltpu.VMEM((16, SRC, HW), BF16),
            pltpu.SemaphoreType.DMA((4,)),
        ]
        + gather_scratch(SRC)
        + scatter_scratch(SRC),
        9 * 10**9,
        enc_tokens,
        src_lengths,
        enc_gain,
        enc_query,
        enc_key,
        enc_value,
        enc_output,
        enc_bias,
        mem_gain,
    )
    hidden = call(
        cross_kernel,
        2,
        jax.ShapeDtypeStruct((TGT, D), F32),
        (VM, VM, SM, SM, VM, VM, pl.ANY, pl.ANY, pl.ANY, pl.ANY),
        weights
        + [
            pltpu.VMEM((TGT, D), F32),
            pltpu.VMEM((16, TGT, HW), BF16),
            pltpu.VMEM((16, TGT, HW), BF16),
            pltpu.SemaphoreType.DMA((4,)),
            pltpu.SemaphoreType.DMA,
            pltpu.SemaphoreType.DMA,
        ]
        + gather_scratch(SRC)
        + gather_scratch(TGT)
        + scatter_scratch(TGT),
        7 * 10**9,
        enc_memory,
        dec_tokens,
        src_lengths,
        lang_tags,
        lang_table,
        cross_gain,
        cross_query,
        cross_key,
        cross_value,
        cross_output,
    )
    dec_out = call(
        ffn_kernel,
        3,
        jax.ShapeDtypeStruct((1, TGT, D), BF16),
        (VM, VM, SM, pl.ANY, pl.ANY),
        [
            pltpu.VMEM((D, FF), BF16),
            pltpu.VMEM((FF, D), BF16),
            pltpu.VMEM((4 * TGT, FF), BF16),
            pltpu.SemaphoreType.DMA((2,)),
        ]
        + gather_scratch(TGT)
        + scatter_scratch(TGT),
        9 * 10**9,
        hidden,
        ffn_gain,
        tgt_lengths,
        ffn_in,
        ffn_out,
    )
    return (enc_memory, dec_out)


def solution(mesh):
    in_specs = (
        P(("dp", "tensor"), None, None),
        P(),
        P(),
        P(None, "tensor"),
        P(None, "tensor"),
        P(None, "tensor"),
        P("tensor", None),
        P("tensor", None),
        P(),
        P(("dp", "tensor"), None, None),
        P(("dp", "tensor")),
        P("dp"),
        P(),
        P(),
        P(None, "tensor"),
        P(None, "tensor"),
        P(None, "tensor"),
        P("tensor", None),
        P(),
        P(None, "tensor"),
        P("tensor", None),
    )
    out_specs = (P(("dp", "tensor"), None, None), P(("dp", "tensor"), None, None))
    return jax.shard_map(
        on_device, mesh=mesh, in_specs=in_specs, out_specs=out_specs, check_vma=False
    )
```

time: 567 us -> 207 us (0.37)
  waiting for transfers between devices: 437 us -> 0 us
  Pallas kernels: 0 us -> 202 us
  matrix products: 67.4 us -> 0 us
  local copies, waits for them, and re-layouts: 24.1 us -> 2.28 us
  other arithmetic: 16.5 us -> 0 us
  between operations: 15.1 us -> 1.32 us
    reduce_scatter x3 -> x0, waiting for transfers between devices: 219 us -> none  [narrow(): lax.psum_scatter(partial_value.astype(jnp.bfloat16), 'tensor', scatter_di...]
    all_gather x4 -> x0, waiting for transfers between devices: 218 us -> none  [widen(): return lax.all_gather(values, 'tensor', axis=0, tiled=True)]
    pallas_call x0 -> x3, Pallas kernels: none -> 202 us  [call(): pl.pallas_call(kernel, out_shape=out_shape, in_specs=[pl.BlockSpec(memory...]
    dot_general x15 -> x0, matrix products: 67.4 us -> none  [the longest x6 27.6 us: project(): jnp.dot(flat_rows, weight, preferred_element_type=jnp.float32)]
    another operation x7 -> x0, local copies, waits for them, and re-layouts: 15.4 us -> none  [the longest x2 6.04 us: attend(): value_heads = value_rows.reshape(examples, key_len, head_count, HD)]
    convert_element_type x5 -> x0, other arithmetic: 7.58 us -> none  [the longest x1 1.79 us: on_device(): enc_normed = rms_norm(enc_input, enc_gain).astype(jnp.bfloat16)]
    reduce_sum x4 -> x0, other arithmetic: 5.75 us -> none  [rms_norm(): mean_sq = jnp.mean(values * values, axis=-1, keepdims=True)]
  transfers between devices with their start and end apart: 8 -> 0, of which waited for: 7 -> 0; matrix products, arithmetic and copies ran while one was open for 2% -> 0% of each run, Pallas kernels for 0% -> 0%
where the time goes in v1:
time: 207 us; the launch traced here: 205 us
  Pallas kernels  202 us (98%)
  local copies, waits for them, and re-layouts  2.28 us (1%)
    pallas_call x3, Pallas kernels, call(): pl.pallas_call(kernel, out_shape=out_shape, in_specs=[pl.BlockSpec(memory...  202 us

profile of v1, /device:TPU:0, one launch (start us, length us, event | category | flops | bytes accessed | tf_op | source)
XLA Modules:
  0.0 205.2 jit_solution(6913228654507521007)
XLA Ops:
  0.6 74.9 %shard_map.212.memory = bf16[1,128,1024]{2,1,0:T(8,128)(2,1)} custom-call(bf16[1,128,1024]{2,1,0:T(8,128)(2,1)} %tokens.2, s32[128]{0:T(128)} %lengths.3, f32[1024]{0:T(1024)} %gain.3, bf16[1024,512]{1,0:T(8,128)(2,1)} %wq_h.2, bf16[1024,512]{1,0:T(8,128)(2,1)} %wk_h.2, bf16[1024,512]{1,0:T(8,128)(2,1)} %wv_h.2, bf16[512,1024]{1,0:T(8,128)(2,1)} %wo_h.2, ...), custom_call_target="tpu_custom_call" | custom-call | flops 8999999488 | bytes 8388608 | tf_op jit(solution)/shard_map/pallas_call | solution.py:582
  75.6 80.8 %shard_map.213.hidden = f32[64,1024]{1,0:T(8,128)} custom-call(bf16[1,128,1024]{2,1,0:T(8,128)(2,1)} %shard_map.212.memory, bf16[1,64,1024]{2,1,0:T(8,128)(2,1)} %tokens.3, s32[128]{0:T(128)} %lengths.3, s32[16]{0:T(128)} %tags.1, bf16[8,1024]{1,0:T(8,128)(2,1)} %table.1, f32[1024]{0:T(1024)} %gain.4, bf16[1024,512]{1,0:T(8,128)(2,1)} %wq_h.3, ...), custom_call_target="tpu_custom_call" | custom-call | flops 7000000000 | bytes 8388608 | tf_op jit(solution)/shard_map/pallas_call | solution.py:582
  157.1 0.0 copy-start
  157.1 45.9 %shard_map.214 = bf16[1,64,1024]{2,1,0:T(8,128)(2,1)} custom-call(f32[64,1024]{1,0:T(8,128)} %shard_map.213.hidden, f32[1024]{0:T(1024)} %gain.5, s32[1]{0:T(128)S(6)} %copy.25.tgt_length, bf16[1024,2048]{1,0:T(8,128)(2,1)} %win_h.1, bf16[2048,1024]{1,0:T(8,128)(2,1)} %wout_h.1), custom_call_target="tpu_custom_call" | custom-call | flops 8999999488 | bytes 8388608 | tf_op jit(solution)/shard_map/pallas_call | solution.py:582
  203.0 0.0 copy-done
  203.0 0.7 copy.26
  203.7 1.6 copy.27
Async XLA Ops:
  157.1 45.9 %copy-start = (bf16[1,128,1024]{2,1,0:T(8,128)(2,1)S(1)}, bf16[1,128,1024]{2,1,0:T(8,128)(2,1)}, u32[]{:S(2)}) copy-start(bf16[1,128,1024]{2,1,0:T(8,128)(2,1)} %shard_map.212.memory) | copy-start | bytes 786436

commit v2 on v0

v2 whole, which is shorter than its diff:
```python
import functools

import jax
import jax.numpy as jnp
from jax import lax
from jax.experimental import pallas as pl
from jax.experimental.pallas import tpu as pltpu
from jax.sharding import PartitionSpec as P

D = 1024
HD = 128
SRC = 128
TGT = 64
MAXREL = 16
NB = 33
LANGS = 8
HEADS = 4
HW = HEADS * HD
FF = 2048
EPSILON = 1e-06
NEG_FILL = -1e30
SCALE = HD ** (-0.5)
MESH = pl.DeviceIdType.MESH
F32 = jnp.float32
BF16 = jnp.bfloat16

GATHER_ORDER = ((0, 0), (0, 1), (0, 3), (1, 0), (0, 2), (1, 1), (1, 3), (1, 2))
SCATTER_ORDER = ((1, 2), (1, 1), (1, 3), (0, 2), (0, 1), (0, 3), (1, 0), (0, 0))
ENC_CHUNKS = 4
MEM_CHUNKS = 2
DEC_CHUNKS = 2


def packed(order):
    return (
        sum(dy << i for i, (dy, dz) in enumerate(order)),
        sum(dz << (2 * i) for i, (dy, dz) in enumerate(order)),
    )


def chip_at(place, order, index):
    dy_bits, dz_bits = packed(order)
    return place.chip((dy_bits >> index) & 1, (dz_bits >> (2 * index)) & 3)


def rms(values, gain):
    mean_sq = jnp.mean(values * values, axis=-1, keepdims=True)
    return values * lax.rsqrt(mean_sq + EPSILON) * gain


class Place:
    def __init__(self):
        self.me = lax.axis_index("tensor")
        self.dp = lax.axis_index("dp")
        self.core = self.me % 2
        self.z = (self.me // 2) % 4
        self.y = self.me // 8
        self.x = self.dp // 2
        self.y_lo = self.dp % 2

    def chip(self, dy, dz):
        return ((self.y + dy) % 2) * 4 + (self.z + dz) % 4

    def slot(self, dy, dz, dk=0):
        return self.chip(dy, dz) * 2 + (self.core + dk) % 2


def send(src, dst, send_sem, recv_sem, device):
    pltpu.make_async_remote_copy(
        src_ref=src,
        dst_ref=dst,
        send_sem=send_sem,
        recv_sem=recv_sem,
        device_id=device,
        device_id_type=MESH,
    ).start()


def arrived(dst, recv_sem):
    pltpu.make_async_copy(dst, dst, recv_sem).wait()


class Gather:
    SENDS = 16

    def __init__(self, place, buf, ssem, rsem, hsem, chunk, chunks):
        self.p, self.buf, self.chunk = place, buf, chunk
        self.ssem, self.rsem, self.hsem = ssem, rsem, hsem
        self.rows = buf.shape[1] // chunks
        self.first = chunk * self.rows
        self.sent = []

    def _part(self, slot):
        return self.buf.at[slot, pl.ds(self.first, self.rows)]

    def _half_part(self, slot, which):
        half = self.rows // 2
        return self.buf.at[slot, pl.ds(self.first + which * half, half)]

    def _send(self, src, recv_sem, target):
        sem = self.ssem.at[self.chunk, len(self.sent)]
        send(src, src, sem, recv_sem, {"tensor": target})
        self.sent.append(src.shape[0])

    def _full(self, slot, target):
        self._send(self._part(slot), self.rsem.at[self.chunk, slot], target)

    def _half(self, slot, which, target):
        self._send(self._half_part(slot, which), self.hsem.at[self.chunk, which], target)

    def start(self):
        p = self.p
        for target in (p.slot(0, 1), p.slot(0, 3), p.slot(1, 0), p.slot(0, 0, 1)):
            self._full(p.me, target)

    def event(self, index):
        p = self.p
        dy, dz = GATHER_ORDER[index]
        slot = p.slot(dy, dz)
        if (dy, dz) == (0, 2):
            for which in (0, 1):
                arrived(self._half_part(slot, which), self.hsem.at[self.chunk, which])
            self._full(slot, p.slot(1, 0))
        else:
            arrived(self._part(slot), self.rsem.at[self.chunk, slot])
        if (dy, dz) == (0, 1):
            self._half(slot, 1, p.slot(0, 3))
        elif (dy, dz) == (0, 3):
            self._half(slot, 0, p.slot(0, 1))
        elif (dy, dz) == (1, 0):
            self._full(slot, p.slot(0, 1))
            self._full(slot, p.slot(0, 3))
        self._full(slot, p.slot(0, 0, 1))

    def partner_wait(self, chip):
        slot = chip * 2 + (self.p.core + 1) % 2
        arrived(self._part(slot), self.rsem.at[self.chunk, slot])

    def drain(self):
        for index, rows in enumerate(self.sent):
            arrived(self.buf.at[0, pl.ds(0, rows)], self.ssem.at[self.chunk, index])

    @staticmethod
    def scratch(rows, chunks):
        return [
            pltpu.VMEM((16, rows, D), BF16),
            pltpu.SemaphoreType.DMA((chunks, Gather.SENDS)),
            pltpu.SemaphoreType.DMA((chunks, 16)),
            pltpu.SemaphoreType.DMA((chunks, 2)),
        ]

    @staticmethod
    def make(place, refs, chunks):
        return [Gather(place, *refs, chunk, chunks) for chunk in range(chunks)]


class Scatter:
    SENDS = 10

    def __init__(self, place, chunks, part, xbuf, yfar, relay, fin, finy, ysend, yrec, *sems):
        self.p, self.chunks = place, chunks
        self.part, self.xbuf, self.yfar, self.relay = part, xbuf, yfar, relay
        self.fin, self.finy, self.ysend, self.yrec = fin, finy, ysend, yrec
        self.psem, self.xsem, self.ssem = sems[:3]
        self.yfar_sem, self.relay_sem, self.fin_sem, self.finy_sem, self.yrec_sem = sems[3:]
        self.rows = part.shape[1] // chunks
        self.half = self.rows // 2
        self.sent = []

    @staticmethod
    def scratch(rows, chunks):
        return [
            pltpu.VMEM((16, rows, D), BF16),
            pltpu.VMEM((8, rows, D), BF16),
            pltpu.VMEM((rows, D), BF16),
            pltpu.VMEM((2, rows // 2, D), BF16),
            pltpu.VMEM((2, rows, D), BF16),
            pltpu.VMEM((2, rows, D), BF16),
            pltpu.VMEM((rows, D), BF16),
            pltpu.VMEM((rows, D), BF16),
            pltpu.SemaphoreType.DMA((8,)),
            pltpu.SemaphoreType.DMA((8,)),
            pltpu.SemaphoreType.DMA((chunks * Scatter.SENDS,)),
            pltpu.SemaphoreType.DMA((chunks,)),
            pltpu.SemaphoreType.DMA((chunks, 2)),
            pltpu.SemaphoreType.DMA((chunks, 2, 2)),
            pltpu.SemaphoreType.DMA((chunks, 2)),
            pltpu.SemaphoreType.DMA((chunks,)),
        ]

    def partner_send(self, chip):
        slot = chip * 2 + (self.p.core + 1) % 2
        send(
            self.part.at[slot],
            self.xbuf.at[chip],
            self.psem.at[chip],
            self.xsem.at[chip],
            {"tensor": self.p.slot(0, 0, 1)},
        )

    def partner_add(self, chip):
        arrived(self.xbuf.at[chip], self.xsem.at[chip])
        slot = chip * 2 + self.p.core
        self.part[slot] = self.part[slot] + self.xbuf[chip]

    def _send(self, src, dst, recv_sem, target):
        sem = self.ssem.at[len(self.sent)]
        send(src, dst, sem, recv_sem, {"tensor": target})
        self.sent.append(src.shape[0])

    def all_rows(self, chunk):
        return pl.ds(chunk * self.rows, self.rows)

    def half_rows(self, chunk, which):
        return pl.ds(chunk * self.rows + which * self.half, self.half)

    def send_yfar(self):
        slot = self.p.slot(1, 2)
        for chunk in range(self.chunks):
            rows = self.all_rows(chunk)
            self._send(
                self.part.at[slot, rows],
                self.yfar.at[rows],
                self.yfar_sem.at[chunk],
                self.p.slot(1, 0),
            )

    def send_side(self, way):
        dz = (1, 3)[way]
        slot = self.p.slot(1, dz)
        for chunk in range(self.chunks):
            rows = self.all_rows(chunk)
            self._send(
                self.part.at[slot, rows],
                self.finy.at[way, rows],
                self.finy_sem.at[chunk, way],
                self.p.slot(0, dz),
            )

    def _near(self, chunk, way, which):
        dz = (1, 3)[way]
        rows = self.half_rows(chunk, which)
        self._send(
            self.part.at[self.p.slot(0, dz), rows],
            self.fin.at[way, rows],
            self.fin_sem.at[chunk, way, which],
            self.p.slot(0, dz),
        )

    def far(self, chunk):
        rows = self.all_rows(chunk)
        slot = self.p.slot(0, 2)
        arrived(self.yfar.at[rows], self.yfar_sem.at[chunk])
        self.part[slot, rows, :] = self.part[slot, rows, :] + self.yfar[rows, :]
        self._near(chunk, 0, 1)
        self._near(chunk, 1, 0)
        for way in (0, 1):
            self._send(
                self.part.at[slot, self.half_rows(chunk, way)],
                self.relay.at[way, pl.ds(chunk * self.half, self.half)],
                self.relay_sem.at[chunk, way],
                self.p.slot(0, (1, 3)[way]),
            )

    def cross_sum(self, chunk):
        rows = self.all_rows(chunk)
        for way in (0, 1):
            arrived(self.finy.at[way, rows], self.finy_sem.at[chunk, way])
        total = self.part[self.p.slot(1, 0), rows, :].astype(F32)
        total = total + self.finy[0, rows, :].astype(F32) + self.finy[1, rows, :].astype(F32)
        self.ysend[rows, :] = total.astype(BF16)

    def cross_send(self, chunk):
        rows = self.all_rows(chunk)
        self._send(
            self.ysend.at[rows], self.yrec.at[rows], self.yrec_sem.at[chunk], self.p.slot(1, 0)
        )

    def relay_add(self, chunk):
        for way in (0, 1):
            here = pl.ds(chunk * self.half, self.half)
            arrived(self.relay.at[way, here], self.relay_sem.at[chunk, way])
            slot, rows = self.p.slot(0, (1, 3)[way]), self.half_rows(chunk, way)
            self.part[slot, rows, :] = self.part[slot, rows, :] + self.relay[way, here, :]

    def relay_send(self, chunk):
        for way in (0, 1):
            self._near(chunk, way, way)

    def total(self, chunk):
        rows = self.all_rows(chunk)
        for way in (0, 1):
            for which in (0, 1):
                arrived(
                    self.fin.at[way, self.half_rows(chunk, which)],
                    self.fin_sem.at[chunk, way, which],
                )
        own = self.part[self.p.me, rows, :].astype(F32)
        own = own + self.fin[0, rows, :].astype(F32) + self.fin[1, rows, :].astype(F32)
        arrived(self.yrec.at[rows], self.yrec_sem.at[chunk])
        return own + self.yrec[rows, :].astype(F32)

    def run(self, *stages):
        steps = (
            self.far,
            self.cross_sum,
            lambda chunk: (self.cross_send(chunk), self.relay_add(chunk)),
            self.relay_send,
        ) + stages
        for time in range(self.chunks + len(steps) - 1):
            for index, stage in enumerate(steps):
                if 0 <= time - index < self.chunks:
                    stage(time - index)

    def drain(self):
        for chip in range(8):
            slot = chip * 2 + (self.p.core + 1) % 2
            arrived(self.part.at[slot], self.psem.at[chip])
        for index, rows in enumerate(self.sent):
            arrived(self.part.at[0, pl.ds(0, rows)], self.ssem.at[index])


def project_out(place, scatter, ctx, weight, also):
    rows = ctx.shape[1]

    def step(index, carry):
        @pl.when(index < 8)
        def _():
            chip = chip_at(place, SCATTER_ORDER, index)
            block = ctx[pl.ds(chip * 2, 2)].reshape(2 * rows, HW)
            scatter.part[pl.ds(chip * 2, 2)] = dot(block, weight[...]).astype(BF16).reshape(2, rows, D)

        @pl.when(jnp.logical_and(index > 0, index < 9))
        def _():
            scatter.partner_send(chip_at(place, SCATTER_ORDER, index - 1))

        @pl.when(index > 1)
        def _():
            scatter.partner_add(chip_at(place, SCATTER_ORDER, index - 2))

        for at, action in also:

            @pl.when(index == at)
            def _(action=action):
                action()

        return carry

    lax.fori_loop(0, 10, step, 0)


def dot(left, right):
    return jnp.dot(left, right, preferred_element_type=F32)


def dot_t(left, right):
    return lax.dot_general(left, right, (((1,), (1,)), ((), ())), preferred_element_type=F32)


def softmax_weights(scores):
    row_max = jnp.max(scores, axis=-1, keepdims=True)
    exponent = jnp.exp(scores - row_max)
    return (exponent * (1.0 / jnp.sum(exponent, axis=-1, keepdims=True))).astype(BF16)


def layer_kernel(*refs):
    refs = list(refs)

    def take(count):
        taken, refs[:count] = refs[:count], []
        return taken

    tokens, lengths, gain, bias, mem_gain = take(5)
    dec_tokens, tags, table, cross_gain, ffn_gain, tgt_length = take(6)
    hbm = take(10)
    memory_out, dec_out = take(2)
    weights = take(10)
    (weight_sem,) = take(1)
    wq, wk, wv, wo, cq, ck, cv, co, win, wout = weights
    grid, q_s, k_s, v_s, s_s, w_s, ctx = take(7)
    hop, hop_sem, swap_sem = take(3)
    inp, q_all, cross_ctx, act, hidden = take(5)
    place = Place()
    enc_refs, mem_refs, dec_refs, ffn_refs = take(4), take(4), take(4), take(4)
    (enc,) = Gather.make(place, enc_refs, 1)
    mem = Gather.make(place, mem_refs, MEM_CHUNKS)
    (dec,) = Gather.make(place, dec_refs, 1)
    ffn = Gather.make(place, ffn_refs, DEC_CHUNKS)
    enc_sum = Scatter(place, ENC_CHUNKS, *take(16))
    cross_sum = Scatter(place, DEC_CHUNKS, *take(16))
    ffn_sum = Scatter(place, DEC_CHUNKS, *take(16))

    loads = [
        pltpu.make_async_copy(src, dst, weight_sem.at[index])
        for index, (src, dst) in enumerate(zip(hbm, weights))
    ]
    shifted_to = place.slot(0, place.x)
    swap_dp = ((place.z + 4 - place.x) % 4) * 2 + place.core
    swap_t = place.y * 8 + place.z * 2 + place.y_lo
    stays = jnp.logical_and(swap_dp == place.dp, swap_t == place.me)
    moves = jnp.logical_not(stays)

    barrier = pltpu.get_barrier_semaphore()
    for target in (
        place.slot(0, 0, 1),
        place.slot(0, 1),
        place.slot(0, 3),
        place.slot(0, 2),
        place.slot(1, 0),
    ):
        pl.semaphore_signal(barrier, inc=1, device_id={"tensor": target}, device_id_type=MESH)

    @pl.when(moves)
    def _():
        pl.semaphore_signal(barrier, inc=1, device_id=(swap_dp, swap_t), device_id_type=MESH)

    enc_buf, mem_buf, dec_buf, ffn_buf = enc_refs[0], mem_refs[0], dec_refs[0], ffn_refs[0]
    enc_buf[place.me] = rms(tokens[0].astype(F32), gain[...]).astype(BF16)
    tag = tags[place.me]
    lang = jnp.zeros((1, D), F32)
    for index in range(LANGS):
        lang = jnp.where(tag == index, table[index : index + 1, :].astype(F32), lang)
    value = dec_tokens[0].astype(F32) + lang
    inp[...] = value
    dec_buf[place.me] = rms(value, cross_gain[...]).astype(BF16)
    for load in loads:
        load.start()

    @pl.when(moves)
    def _():
        pl.semaphore_wait(barrier, 6)

    @pl.when(stays)
    def _():
        pl.semaphore_wait(barrier, 5)

    enc.start()

    keys = lax.broadcasted_iota(jnp.int32, (SRC, SRC), 1)
    bucket = jnp.clip(keys - lax.broadcasted_iota(jnp.int32, (SRC, SRC), 0), -MAXREL, MAXREL) + MAXREL
    for head in range(HEADS):
        values = jnp.zeros((SRC, SRC), F32)
        for index in range(NB):
            values = jnp.where(bucket == index, bias[head, index], values)
        grid[head] = values
    for load in loads[:4]:
        load.wait()

    items = [(ex, head) for ex in range(2) for head in range(HEADS)]

    def enc_step(index, carry):
        @pl.when(index == 1)
        def _():
            for event in (1, 2, 3):
                enc.event(event)

        @pl.when(index == 4)
        def _():
            for event in (4, 5, 6):
                enc.event(event)

        @pl.when(index == 6)
        def _():
            dec.start()

        @pl.when(index == 7)
        def _():
            enc.event(7)

        chip = chip_at(place, GATHER_ORDER, index)
        enc.partner_wait(chip)
        rows = enc_buf[pl.ds(chip * 2, 2)].reshape(2 * SRC, D)
        q_s[...] = dot(rows, wq[...]).astype(BF16)
        k_s[...] = dot(rows, wk[...]).astype(BF16)
        v_s[...] = dot(rows, wv[...]).astype(BF16)
        columns = lax.broadcasted_iota(jnp.int32, (SRC, SRC), 1)
        for item, (ex, head) in enumerate(items):
            here, cols = slice(ex * SRC, (ex + 1) * SRC), slice(head * HD, (head + 1) * HD)
            s_s[item] = dot_t(q_s[here, cols], k_s[here, cols])
        for item, (ex, head) in enumerate(items):
            length = lengths[place.dp * 16 + chip * 2 + ex]
            scores = s_s[item] * SCALE + grid[head]
            w_s[item] = softmax_weights(jnp.where(columns < length, scores, NEG_FILL))
        for item, (ex, head) in enumerate(items):
            here, cols = slice(ex * SRC, (ex + 1) * SRC), slice(head * HD, (head + 1) * HD)
            ctx[chip * 2 + ex, :, cols] = dot(w_s[item], v_s[here, cols]).astype(BF16)
        return carry

    lax.fori_loop(0, 8, enc_step, 0)

    def dec_events(*events):
        def action():
            for event in events:
                dec.event(event)

        return action

    project_out(
        place,
        enc_sum,
        ctx,
        wo,
        (
            (1, dec_events(1, 2, 3)),
            (3, enc_sum.send_yfar),
            (4, functools.partial(enc_sum.send_side, 0)),
            (5, functools.partial(enc_sum.send_side, 1)),
            (9, dec_events(4, 5, 6, 7)),
        ),
    )

    def finish_memory(chunk):
        rows = enc_sum.all_rows(chunk)
        value = tokens[0, rows, :].astype(F32) + enc_sum.total(chunk)
        memory_out[0, rows, :] = rms(value, mem_gain[...]).astype(BF16)

    def shift_send(chunk):
        rows = enc_sum.all_rows(chunk)

        @pl.when(place.x == 0)
        def _():
            pltpu.make_async_copy(memory_out.at[0, rows], hop.at[rows], hop_sem.at[1, chunk]).start()

        @pl.when(place.x > 0)
        def _():
            send(
                memory_out.at[0, rows],
                hop.at[rows],
                hop_sem.at[0, chunk],
                hop_sem.at[1, chunk],
                {"tensor": shifted_to},
            )

    def swap_send(chunk):
        rows = enc_sum.all_rows(chunk)
        arrived(hop.at[rows], hop_sem.at[1, chunk])

        @pl.when(stays)
        def _():
            pltpu.make_async_copy(
                hop.at[rows], mem_buf.at[place.me, rows], swap_sem.at[1, chunk]
            ).start()

        @pl.when(moves)
        def _():
            send(
                hop.at[rows],
                mem_buf.at[swap_t, rows],
                swap_sem.at[0, chunk],
                swap_sem.at[1, chunk],
                (swap_dp, swap_t),
            )

    def spread(chunk):
        rows = enc_sum.all_rows(chunk)
        arrived(mem_buf.at[place.me, rows], swap_sem.at[1, chunk])
        each = ENC_CHUNKS // MEM_CHUNKS
        if chunk % each == each - 1:
            mem[chunk // each].start()

    enc_sum.run(finish_memory, shift_send, swap_send, spread)

    for chip in range(8):
        dec.partner_wait(chip)
    for load in loads[4:8]:
        load.wait()

    def q_step(index, carry):
        rows = dec_buf[pl.ds(index * 4, 4)].reshape(4 * TGT, D)
        q_all[pl.ds(index * 4, 4)] = dot(rows, cq[...]).astype(BF16).reshape(4, TGT, HW)
        return carry

    lax.fori_loop(0, 4, q_step, 0)

    def cross_step(index, carry):
        @pl.when(index == 1)
        def _():
            for gather in mem:
                for event in (1, 2, 3):
                    gather.event(event)

        @pl.when(index == 4)
        def _():
            for gather in mem:
                for event in (4, 5, 6):
                    gather.event(event)

        @pl.when(index == 7)
        def _():
            for gather in mem:
                gather.event(7)

        chip = chip_at(place, GATHER_ORDER, index)
        for gather in mem:
            gather.partner_wait(chip)
        rows = mem_buf[pl.ds(chip * 2, 2)].reshape(2 * SRC, D)
        k_s[...] = dot(rows, ck[...]).astype(BF16)
        v_s[...] = dot(rows, cv[...]).astype(BF16)
        columns = lax.broadcasted_iota(jnp.int32, (TGT, SRC), 1)
        base = ((chip % 4 + 4 - place.x) % 4) * 4 + chip // 4
        for item, (ex, head) in enumerate(items):
            here, cols = slice(ex * SRC, (ex + 1) * SRC), slice(head * HD, (head + 1) * HD)
            s_s[item, :TGT, :] = dot_t(q_all[base + 2 * ex, :, cols], k_s[here, cols])
        for item, (ex, head) in enumerate(items):
            row = base + 2 * ex
            length = lengths[(row // 2) * 16 + (row % 2) * 8 + place.dp]
            scores = s_s[item, :TGT, :] * SCALE
            w_s[item, :TGT, :] = softmax_weights(jnp.where(columns < length, scores, NEG_FILL))
        for item, (ex, head) in enumerate(items):
            here, cols = slice(ex * SRC, (ex + 1) * SRC), slice(head * HD, (head + 1) * HD)
            cross_ctx[base + 2 * ex, :, cols] = dot(w_s[item, :TGT, :], v_s[here, cols]).astype(BF16)
        return carry

    lax.fori_loop(0, 8, cross_step, 0)
    project_out(
        place,
        cross_sum,
        cross_ctx,
        co,
        (
            (3, cross_sum.send_yfar),
            (4, functools.partial(cross_sum.send_side, 0)),
            (5, functools.partial(cross_sum.send_side, 1)),
        ),
    )

    def finish_hidden(chunk):
        rows = cross_sum.all_rows(chunk)
        value = inp[rows, :] + cross_sum.total(chunk)
        hidden[rows, :] = value
        ffn_buf[place.me, rows, :] = rms(value, ffn_gain[...]).astype(BF16)

    cross_sum.run(finish_hidden, lambda chunk: ffn[chunk].start())
    for load in loads[8:]:
        load.wait()

    def ffn_step(index, carry):
        for pair in range(4):

            @pl.when(index == pair)
            def _(pair=pair):
                for gather in ffn:
                    for event in (2 * pair, 2 * pair + 1):
                        if event > 0:
                            gather.event(event)

        first = chip_at(place, GATHER_ORDER, index * 2)
        second = chip_at(place, GATHER_ORDER, index * 2 + 1)
        for gather in ffn:
            gather.partner_wait(first)
            gather.partner_wait(second)
        rows = jnp.concatenate(
            [
                ffn_buf[pl.ds(first * 2, 2)].reshape(2 * TGT, D),
                ffn_buf[pl.ds(second * 2, 2)].reshape(2 * TGT, D),
            ],
            axis=0,
        )
        for tile in range(FF // 512):
            cols = slice(tile * 512, (tile + 1) * 512)
            act[:, cols] = jnp.maximum(dot(rows, win[:, cols]), 0.0).astype(BF16)
        for tile in range(D // 256):
            cols = slice(tile * 256, (tile + 1) * 256)
            result = dot(act[...], wout[:, cols]).astype(BF16)
            ffn_sum.part[pl.ds(first * 2, 2), :, cols] = result[: 2 * TGT].reshape(2, TGT, 256)
            ffn_sum.part[pl.ds(second * 2, 2), :, cols] = result[2 * TGT :].reshape(2, TGT, 256)

        @pl.when(index > 0)
        def _():
            ffn_sum.partner_send(chip_at(place, GATHER_ORDER, index * 2 - 2))
            ffn_sum.partner_send(chip_at(place, GATHER_ORDER, index * 2 - 1))

        return carry

    lax.fori_loop(0, 4, ffn_step, 0)
    ffn_sum.partner_send(place.chip(*GATHER_ORDER[6]))
    ffn_sum.partner_send(place.chip(*GATHER_ORDER[7]))
    for index in range(8):
        ffn_sum.partner_add(place.chip(*SCATTER_ORDER[index]))
        if index == 0:
            ffn_sum.send_yfar()
        elif index < 3:
            ffn_sum.send_side(index - 1)

    def finish_out(chunk):
        rows = ffn_sum.all_rows(chunk)
        value = hidden[rows, :] + ffn_sum.total(chunk)
        position = lax.broadcasted_iota(jnp.int32, value.shape, 0) + chunk * ffn_sum.rows
        dec_out[0, rows, :] = jnp.where(position < tgt_length[0], value, 0.0).astype(BF16)

    ffn_sum.run(finish_out)

    for chunk in range(ENC_CHUNKS):
        rows = enc_sum.all_rows(chunk)

        @pl.when(place.x > 0)
        def _(rows=rows, chunk=chunk):
            arrived(hop.at[rows], hop_sem.at[0, chunk])

        @pl.when(moves)
        def _(rows=rows, chunk=chunk):
            arrived(hop.at[rows], swap_sem.at[0, chunk])

    for stage in [enc, dec, *mem, *ffn, enc_sum, cross_sum, ffn_sum]:
        stage.drain()


VM = pltpu.VMEM
SM = pltpu.SMEM


def on_device(
    enc_tokens,
    src_lengths,
    enc_gain,
    enc_query,
    enc_key,
    enc_value,
    enc_output,
    enc_bias,
    mem_gain,
    dec_tokens,
    tgt_lengths,
    lang_tags,
    lang_table,
    cross_gain,
    cross_query,
    cross_key,
    cross_value,
    cross_output,
    ffn_gain,
    ffn_in,
    ffn_out,
):
    weights = [
        enc_query,
        enc_key,
        enc_value,
        enc_output,
        cross_query,
        cross_key,
        cross_value,
        cross_output,
        ffn_in,
        ffn_out,
    ]
    spaces = [VM, SM, VM, SM, VM, VM, SM, VM, VM, VM, SM] + [pl.ANY] * len(weights)
    scratch = [pltpu.VMEM(weight.shape, BF16) for weight in weights]
    scratch += [
        pltpu.SemaphoreType.DMA((len(weights),)),
        pltpu.VMEM((HEADS, SRC, SRC), F32),
        pltpu.VMEM((2 * SRC, HW), BF16),
        pltpu.VMEM((2 * SRC, HW), BF16),
        pltpu.VMEM((2 * SRC, HW), BF16),
        pltpu.VMEM((2 * HEADS, SRC, SRC), F32),
        pltpu.VMEM((2 * HEADS, SRC, SRC), BF16),
        pltpu.VMEM((16, SRC, HW), BF16),
        pltpu.VMEM((SRC, D), BF16),
        pltpu.SemaphoreType.DMA((2, ENC_CHUNKS)),
        pltpu.SemaphoreType.DMA((2, ENC_CHUNKS)),
        pltpu.VMEM((TGT, D), F32),
        pltpu.VMEM((16, TGT, HW), BF16),
        pltpu.VMEM((16, TGT, HW), BF16),
        pltpu.VMEM((4 * TGT, FF), BF16),
        pltpu.VMEM((TGT, D), F32),
    ]
    scratch += Gather.scratch(SRC, 1)
    scratch += Gather.scratch(SRC, MEM_CHUNKS)
    scratch += Gather.scratch(TGT, 1)
    scratch += Gather.scratch(TGT, DEC_CHUNKS)
    scratch += Scatter.scratch(SRC, ENC_CHUNKS)
    scratch += Scatter.scratch(TGT, DEC_CHUNKS)
    scratch += Scatter.scratch(TGT, DEC_CHUNKS)
    return pl.pallas_call(
        layer_kernel,
        out_shape=(
            jax.ShapeDtypeStruct((1, SRC, D), BF16),
            jax.ShapeDtypeStruct((1, TGT, D), BF16),
        ),
        in_specs=[pl.BlockSpec(memory_space=space) for space in spaces],
        out_specs=(pl.BlockSpec(memory_space=VM), pl.BlockSpec(memory_space=VM)),
        scratch_shapes=scratch,
        compiler_params=pltpu.CompilerParams(
            collective_id=1, has_side_effects=True, vmem_limit_bytes=67_043_328
        ),
    )(
        enc_tokens,
        src_lengths,
        enc_gain,
        enc_bias,
        mem_gain,
        dec_tokens,
        lang_tags,
        lang_table,
        cross_gain,
        ffn_gain,
        tgt_lengths,
        *weights,
    )


def solution(mesh):
    in_specs = (
        P(("dp", "tensor"), None, None),
        P(),
        P(),
        P(None, "tensor"),
        P(None, "tensor"),
        P(None, "tensor"),
        P("tensor", None),
        P("tensor", None),
        P(),
        P(("dp", "tensor"), None, None),
        P(("dp", "tensor")),
        P("dp"),
        P(),
        P(),
        P(None, "tensor"),
        P(None, "tensor"),
        P(None, "tensor"),
        P("tensor", None),
        P(),
        P(None, "tensor"),
        P("tensor", None),
    )
    out_specs = (P(("dp", "tensor"), None, None), P(("dp", "tensor"), None, None))
    return jax.shard_map(
        on_device, mesh=mesh, in_specs=in_specs, out_specs=out_specs, check_vma=False
    )
```

time: 567 us -> 158 us (0.28)
  waiting for transfers between devices: 437 us -> 0 us
  Pallas kernels: 0 us -> 154 us
  matrix products: 67.4 us -> 0 us
  local copies, waits for them, and re-layouts: 24.1 us -> 3.24 us
  other arithmetic: 16.5 us -> 0 us
  between operations: 15.1 us -> 1.29 us
    reduce_scatter x3 -> x0, waiting for transfers between devices: 219 us -> none  [narrow(): lax.psum_scatter(partial_value.astype(jnp.bfloat16), 'tensor', scatter_di...]
    all_gather x4 -> x0, waiting for transfers between devices: 218 us -> none  [widen(): return lax.all_gather(values, 'tensor', axis=0, tiled=True)]
    pallas_call x0 -> x1, Pallas kernels: none -> 154 us  [on_device(): pl.pallas_call(layer_kernel, out_shape=(jax.ShapeDtypeStruct((1, SRC, D),...]
    dot_general x15 -> x0, matrix products: 67.4 us -> none  [the longest x6 27.6 us: project(): jnp.dot(flat_rows, weight, preferred_element_type=jnp.float32)]
    another operation x7 -> x0, local copies, waits for them, and re-layouts: 15.4 us -> none  [the longest x2 6.04 us: attend(): value_heads = value_rows.reshape(examples, key_len, head_count, HD)]
    convert_element_type x5 -> x0, other arithmetic: 7.58 us -> none  [the longest x1 1.79 us: on_device(): enc_normed = rms_norm(enc_input, enc_gain).astype(jnp.bfloat16)]
    reduce_sum x4 -> x0, other arithmetic: 5.75 us -> none  [rms_norm(): mean_sq = jnp.mean(values * values, axis=-1, keepdims=True)]
  transfers between devices with their start and end apart: 8 -> 0, of which waited for: 7 -> 0; matrix products, arithmetic and copies ran while one was open for 2% -> 0% of each run, Pallas kernels for 0% -> 0%
where the time goes in v2:
time: 158 us
  Pallas kernels  154 us (97%)
  local copies, waits for them, and re-layouts  3.24 us (2%)
    pallas_call x1, Pallas kernels, on_device(): pl.pallas_call(layer_kernel, out_shape=(jax.ShapeDtypeStruct((1, SRC, D),...  154 us
    unnamed x2, local copies, waits for them, and re-layouts  3.24 us

profile of v2, /device:TPU:0, one launch (start us, length us, event | category | flops | bytes accessed | tf_op | source)
XLA Modules:
  0.0 158.2 jit_solution(14129827178760162555)
XLA Ops:
  1.3 153.7 %shard_map.212 = (bf16[1,128,1024]{2,1,0:T(8,128)(2,1)}, bf16[1,64,1024]{2,1,0:T(8,128)(2,1)}) custom-call(bf16[1,128,1024]{2,1,0:T(8,128)(2,1)} %refs_0_.1, s32[128]{0:T(128)} %refs_1_.1, f32[1024]{0:T(1024)} %refs_2_.1, f32[4,33]{1,0:T(4,128)} %refs_3_.1, f32[1024]{0:T(1024)} %refs_4_.1, bf16[1,64,1024]{2,1,0:T(8,128)(2,1)} %refs_5_.1, s32[16]{0:T(128)} %refs_6_.1, ...), custom_call_target="tpu_custom_call" | custom-call | tf_op jit(solution)/shard_map/pallas_call | solution.py:774
  155.0 1.7 %copy.26 = bf16[1,128,1024]{2,1,0:T(8,128)(2,1)} copy(bf16[1,128,1024]{2,1,0:T(8,128)(2,1)} %get-tuple-element.4) | data formatting | bytes 524288
  156.6 1.6 copy.27

commit v3 on v2

--- a/solution.py
+++ b/solution.py
@@ -26,6 +26,8 @@
 
 GATHER_ORDER = ((0, 0), (0, 1), (0, 3), (1, 0), (0, 2), (1, 1), (1, 3), (1, 2))
 SCATTER_ORDER = ((1, 2), (1, 1), (1, 3), (0, 2), (0, 1), (0, 3), (1, 0), (0, 0))
+FFN_ORDER = ((0, 0), (0, 1), (1, 2), (0, 2), (1, 1), (1, 3), (1, 0), (0, 3))
+ROW_CHUNKS = 2
 ENC_CHUNKS = 4
 MEM_CHUNKS = 2
 DEC_CHUNKS = 2
@@ -83,8 +85,8 @@
 class Gather:
     SENDS = 16
 
-    def __init__(self, place, buf, ssem, rsem, hsem, chunk, chunks):
-        self.p, self.buf, self.chunk = place, buf, chunk
+    def __init__(self, place, buf, ssem, rsem, hsem, chunk, chunks, direct):
+        self.p, self.buf, self.chunk, self.direct = place, buf, chunk, direct
         self.ssem, self.rsem, self.hsem = ssem, rsem, hsem
         self.rows = buf.shape[1] // chunks
         self.first = chunk * self.rows
@@ -112,20 +114,23 @@
         p = self.p
         for target in (p.slot(0, 1), p.slot(0, 3), p.slot(1, 0), p.slot(0, 0, 1)):
             self._full(p.me, target)
+        if self.direct:
+            self._full(p.me, p.slot(0, 2))
 
     def event(self, index):
         p = self.p
         dy, dz = GATHER_ORDER[index]
         slot = p.slot(dy, dz)
-        if (dy, dz) == (0, 2):
+        if (dy, dz) == (0, 2) and not self.direct:
             for which in (0, 1):
                 arrived(self._half_part(slot, which), self.hsem.at[self.chunk, which])
-            self._full(slot, p.slot(1, 0))
         else:
             arrived(self._part(slot), self.rsem.at[self.chunk, slot])
-        if (dy, dz) == (0, 1):
+        if (dy, dz) == (0, 2):
+            self._full(slot, p.slot(1, 0))
+        elif (dy, dz) == (0, 1) and not self.direct:
             self._half(slot, 1, p.slot(0, 3))
-        elif (dy, dz) == (0, 3):
+        elif (dy, dz) == (0, 3) and not self.direct:
             self._half(slot, 0, p.slot(0, 1))
         elif (dy, dz) == (1, 0):
             self._full(slot, p.slot(0, 1))
@@ -150,15 +155,15 @@
         ]
 
     @staticmethod
-    def make(place, refs, chunks):
-        return [Gather(place, *refs, chunk, chunks) for chunk in range(chunks)]
+    def make(place, refs, chunks, direct=False):
+        return [Gather(place, *refs, chunk, chunks, direct) for chunk in range(chunks)]
 
 
 class Scatter:
     SENDS = 10
 
-    def __init__(self, place, chunks, part, xbuf, yfar, relay, fin, finy, ysend, yrec, *sems):
-        self.p, self.chunks = place, chunks
+    def __init__(self, place, chunks, direct, part, xbuf, yfar, relay, fin, finy, ysend, yrec, *sems):
+        self.p, self.chunks, self.direct = place, chunks, direct
         self.part, self.xbuf, self.yfar, self.relay = part, xbuf, yfar, relay
         self.fin, self.finy, self.ysend, self.yrec = fin, finy, ysend, yrec
         self.psem, self.xsem, self.ssem = sems[:3]
@@ -173,7 +178,7 @@
             pltpu.VMEM((16, rows, D), BF16),
             pltpu.VMEM((8, rows, D), BF16),
             pltpu.VMEM((rows, D), BF16),
-            pltpu.VMEM((2, rows // 2, D), BF16),
+            pltpu.VMEM((rows, D), BF16),
             pltpu.VMEM((2, rows, D), BF16),
             pltpu.VMEM((2, rows, D), BF16),
             pltpu.VMEM((rows, D), BF16),
@@ -247,17 +252,27 @@
             self.p.slot(0, dz),
         )
 
+    def send_near(self, way):
+        for chunk in range(self.chunks):
+            for which in (0, 1):
+                self._near(chunk, way, which)
+
     def far(self, chunk):
         rows = self.all_rows(chunk)
         slot = self.p.slot(0, 2)
         arrived(self.yfar.at[rows], self.yfar_sem.at[chunk])
         self.part[slot, rows, :] = self.part[slot, rows, :] + self.yfar[rows, :]
+        if self.direct:
+            self._send(
+                self.part.at[slot, rows], self.relay.at[rows], self.relay_sem.at[chunk, 0], slot
+            )
+            return
         self._near(chunk, 0, 1)
         self._near(chunk, 1, 0)
         for way in (0, 1):
             self._send(
                 self.part.at[slot, self.half_rows(chunk, way)],
-                self.relay.at[way, pl.ds(chunk * self.half, self.half)],
+                self.relay.at[self.half_rows(chunk, way)],
                 self.relay_sem.at[chunk, way],
                 self.p.slot(0, (1, 3)[way]),
             )
@@ -278,10 +293,9 @@
 
     def relay_add(self, chunk):
         for way in (0, 1):
-            here = pl.ds(chunk * self.half, self.half)
-            arrived(self.relay.at[way, here], self.relay_sem.at[chunk, way])
             slot, rows = self.p.slot(0, (1, 3)[way]), self.half_rows(chunk, way)
-            self.part[slot, rows, :] = self.part[slot, rows, :] + self.relay[way, here, :]
+            arrived(self.relay.at[rows], self.relay_sem.at[chunk, way])
+            self.part[slot, rows, :] = self.part[slot, rows, :] + self.relay[rows, :]
 
     def relay_send(self, chunk):
         for way in (0, 1):
@@ -297,16 +311,22 @@
                 )
         own = self.part[self.p.me, rows, :].astype(F32)
         own = own + self.fin[0, rows, :].astype(F32) + self.fin[1, rows, :].astype(F32)
+        if self.direct:
+            arrived(self.relay.at[rows], self.relay_sem.at[chunk, 0])
+            own = own + self.relay[rows, :].astype(F32)
         arrived(self.yrec.at[rows], self.yrec_sem.at[chunk])
         return own + self.yrec[rows, :].astype(F32)
 
     def run(self, *stages):
-        steps = (
-            self.far,
-            self.cross_sum,
-            lambda chunk: (self.cross_send(chunk), self.relay_add(chunk)),
-            self.relay_send,
-        ) + stages
+        if self.direct:
+            steps = (self.cross_sum, self.cross_send) + stages
+        else:
+            steps = (
+                self.far,
+                self.cross_sum,
+                lambda chunk: (self.cross_send(chunk), self.relay_add(chunk)),
+                self.relay_send,
+            ) + stages
         for time in range(self.chunks + len(steps) - 1):
             for index, stage in enumerate(steps):
                 if 0 <= time - index < self.chunks:
@@ -382,13 +402,18 @@
     inp, q_all, cross_ctx, act, hidden = take(5)
     place = Place()
     enc_refs, mem_refs, dec_refs, ffn_refs = take(4), take(4), take(4), take(4)
-    (enc,) = Gather.make(place, enc_refs, 1)
+    enc = Gather.make(place, enc_refs, ROW_CHUNKS)
     mem = Gather.make(place, mem_refs, MEM_CHUNKS)
     (dec,) = Gather.make(place, dec_refs, 1)
-    ffn = Gather.make(place, ffn_refs, DEC_CHUNKS)
-    enc_sum = Scatter(place, ENC_CHUNKS, *take(16))
-    cross_sum = Scatter(place, DEC_CHUNKS, *take(16))
-    ffn_sum = Scatter(place, DEC_CHUNKS, *take(16))
+    ffn = Gather.make(place, ffn_refs, DEC_CHUNKS, True)
+    enc_sum = Scatter(place, ENC_CHUNKS, False, *take(16))
+    cross_sum = Scatter(place, DEC_CHUNKS, True, *take(16))
+    ffn_sum = Scatter(place, DEC_CHUNKS, True, *take(16))
+
+    def events(gathers, *numbers):
+        for gather in gathers:
+            for number in numbers:
+                gather.event(number)
 
     loads = [
         pltpu.make_async_copy(src, dst, weight_sem.at[index])
@@ -423,7 +448,7 @@
     value = dec_tokens[0].astype(F32) + lang
     inp[...] = value
     dec_buf[place.me] = rms(value, cross_gain[...]).astype(BF16)
-    for load in loads:
+    for load in loads[:4]:
         load.start()
 
     @pl.when(moves)
@@ -434,7 +459,8 @@
     def _():
         pl.semaphore_wait(barrier, 5)
 
-    enc.start()
+    for gather in enc:
+        gather.start()
 
     keys = lax.broadcasted_iota(jnp.int32, (SRC, SRC), 1)
     bucket = jnp.clip(keys - lax.broadcasted_iota(jnp.int32, (SRC, SRC), 0), -MAXREL, MAXREL) + MAXREL
@@ -451,24 +477,26 @@
     def enc_step(index, carry):
         @pl.when(index == 1)
         def _():
-            for event in (1, 2, 3):
-                enc.event(event)
+            events(enc, 1, 2, 3)
+            dec.start()
+            for load in loads[4:]:
+                load.start()
 
         @pl.when(index == 4)
         def _():
-            for event in (4, 5, 6):
-                enc.event(event)
-
-        @pl.when(index == 6)
-        def _():
-            dec.start()
+            events(enc, 4, 5, 6)
+
+        @pl.when(index == 5)
+        def _():
+            events([dec], 1, 2, 3)
 
         @pl.when(index == 7)
         def _():
-            enc.event(7)
+            events(enc, 7)
 
         chip = chip_at(place, GATHER_ORDER, index)
-        enc.partner_wait(chip)
+        for gather in enc:
+            gather.partner_wait(chip)
         rows = enc_buf[pl.ds(chip * 2, 2)].reshape(2 * SRC, D)
         q_s[...] = dot(rows, wq[...]).astype(BF16)
         k_s[...] = dot(rows, wk[...]).astype(BF16)
@@ -488,24 +516,16 @@
 
     lax.fori_loop(0, 8, enc_step, 0)
 
-    def dec_events(*events):
-        def action():
-            for event in events:
-                dec.event(event)
-
-        return action
-
     project_out(
         place,
         enc_sum,
         ctx,
         wo,
         (
-            (1, dec_events(1, 2, 3)),
+            (1, functools.partial(events, [dec], 4, 5, 6, 7)),
             (3, enc_sum.send_yfar),
             (4, functools.partial(enc_sum.send_side, 0)),
             (5, functools.partial(enc_sum.send_side, 1)),
-            (9, dec_events(4, 5, 6, 7)),
         ),
     )
 
@@ -575,20 +595,15 @@
     def cross_step(index, carry):
         @pl.when(index == 1)
         def _():
-            for gather in mem:
-                for event in (1, 2, 3):
-                    gather.event(event)
+            events(mem, 1, 2, 3)
 
         @pl.when(index == 4)
         def _():
-            for gather in mem:
-                for event in (4, 5, 6):
-                    gather.event(event)
+            events(mem, 4, 5, 6)
 
         @pl.when(index == 7)
         def _():
-            for gather in mem:
-                gather.event(7)
+            events(mem, 7)
 
         chip = chip_at(place, GATHER_ORDER, index)
         for gather in mem:
@@ -621,6 +636,9 @@
             (3, cross_sum.send_yfar),
             (4, functools.partial(cross_sum.send_side, 0)),
             (5, functools.partial(cross_sum.send_side, 1)),
+            (7, functools.partial(cross_sum.send_near, 0)),
+            (8, functools.partial(cross_sum.send_near, 1)),
+            (9, lambda: [cross_sum.far(chunk) for chunk in range(DEC_CHUNKS)]),
         ),
     )
 
@@ -635,20 +653,29 @@
         load.wait()
 
     def ffn_step(index, carry):
-        for pair in range(4):
-
-            @pl.when(index == pair)
-            def _(pair=pair):
+        @pl.when(index == 0)
+        def _():
+            events(ffn, 1, 2, 3, 4)
+
+        @pl.when(index == 1)
+        def _():
+            events(ffn, 5, 6, 7)
+
+        first = chip_at(place, FFN_ORDER, index * 2)
+        second = chip_at(place, FFN_ORDER, index * 2 + 1)
+
+        @pl.when(index == 0)
+        def _():
+            for chip in range(2):
                 for gather in ffn:
-                    for event in (2 * pair, 2 * pair + 1):
-                        if event > 0:
-                            gather.event(event)
-
-        first = chip_at(place, GATHER_ORDER, index * 2)
-        second = chip_at(place, GATHER_ORDER, index * 2 + 1)
-        for gather in ffn:
-            gather.partner_wait(first)
-            gather.partner_wait(second)
+                    gather.partner_wait(place.chip(*FFN_ORDER[chip]))
+
+        @pl.when(index == 1)
+        def _():
+            for chip in range(2, 8):
+                for gather in ffn:
+                    gather.partner_wait(place.chip(*FFN_ORDER[chip]))
+
         rows = jnp.concatenate(
             [
                 ffn_buf[pl.ds(first * 2, 2)].reshape(2 * TGT, D),
@@ -659,28 +686,40 @@
         for tile in range(FF // 512):
             cols = slice(tile * 512, (tile + 1) * 512)
             act[:, cols] = jnp.maximum(dot(rows, win[:, cols]), 0.0).astype(BF16)
+
+        @pl.when(index > 0)
+        def _():
+            ffn_sum.partner_add(chip_at(place, FFN_ORDER, index * 2 - 2))
+            ffn_sum.partner_add(chip_at(place, FFN_ORDER, index * 2 - 1))
+
+        @pl.when(index == 1)
+        def _():
+            ffn_sum.send_near(0)
+
+        @pl.when(index == 2)
+        def _():
+            ffn_sum.send_yfar()
+
+        @pl.when(index == 3)
+        def _():
+            ffn_sum.send_side(0)
+            ffn_sum.send_side(1)
+            for chunk in range(DEC_CHUNKS):
+                ffn_sum.far(chunk)
+
         for tile in range(D // 256):
             cols = slice(tile * 256, (tile + 1) * 256)
             result = dot(act[...], wout[:, cols]).astype(BF16)
             ffn_sum.part[pl.ds(first * 2, 2), :, cols] = result[: 2 * TGT].reshape(2, TGT, 256)
             ffn_sum.part[pl.ds(second * 2, 2), :, cols] = result[2 * TGT :].reshape(2, TGT, 256)
-
-        @pl.when(index > 0)
-        def _():
-            ffn_sum.partner_send(chip_at(place, GATHER_ORDER, index * 2 - 2))
-            ffn_sum.partner_send(chip_at(place, GATHER_ORDER, index * 2 - 1))
-
+        ffn_sum.partner_send(first)
+        ffn_sum.partner_send(second)
         return carry
 
     lax.fori_loop(0, 4, ffn_step, 0)
-    ffn_sum.partner_send(place.chip(*GATHER_ORDER[6]))
-    ffn_sum.partner_send(place.chip(*GATHER_ORDER[7]))
-    for index in range(8):
-        ffn_sum.partner_add(place.chip(*SCATTER_ORDER[index]))
-        if index == 0:
-            ffn_sum.send_yfar()
-        elif index < 3:
-            ffn_sum.send_side(index - 1)
+    for index in (6, 7):
+        ffn_sum.partner_add(place.chip(*FFN_ORDER[index]))
+    ffn_sum.send_near(1)
 
     def finish_out(chunk):
         rows = ffn_sum.all_rows(chunk)
@@ -701,8 +740,13 @@
         def _(rows=rows, chunk=chunk):
             arrived(hop.at[rows], swap_sem.at[0, chunk])
 
-    for stage in [enc, dec, *mem, *ffn, enc_sum, cross_sum, ffn_sum]:
+    for stage in [*enc, dec, *mem, *ffn, enc_sum, cross_sum, ffn_sum]:
         stage.drain()
+
+
+def leave_kernel(memory, dec, memory_out, dec_out):
+    memory_out[...] = memory[...]
+    dec_out[...] = dec[...]
 
 
 VM = pltpu.VMEM
@@ -764,14 +808,14 @@
         pltpu.VMEM((4 * TGT, FF), BF16),
         pltpu.VMEM((TGT, D), F32),
     ]
-    scratch += Gather.scratch(SRC, 1)
+    scratch += Gather.scratch(SRC, ROW_CHUNKS)
     scratch += Gather.scratch(SRC, MEM_CHUNKS)
     scratch += Gather.scratch(TGT, 1)
     scratch += Gather.scratch(TGT, DEC_CHUNKS)
     scratch += Scatter.scratch(SRC, ENC_CHUNKS)
     scratch += Scatter.scratch(TGT, DEC_CHUNKS)
     scratch += Scatter.scratch(TGT, DEC_CHUNKS)
-    return pl.pallas_call(
+    memory, dec = pl.pallas_call(
         layer_kernel,
         out_shape=(
             jax.ShapeDtypeStruct((1, SRC, D), BF16),
@@ -797,6 +841,15 @@
         tgt_lengths,
         *weights,
     )
+    return pl.pallas_call(
+        leave_kernel,
+        out_shape=(
+            jax.ShapeDtypeStruct(memory.shape, BF16),
+            jax.ShapeDtypeStruct(dec.shape, BF16),
+        ),
+        in_specs=[pl.BlockSpec(memory_space=VM)] * 2,
+        out_specs=(pl.BlockSpec(memory_space=VM), pl.BlockSpec(memory_space=VM)),
+    )(memory, dec)
 
 
 def solution(mesh):

time: 158 us -> 153 us (0.968)
  local copies, waits for them, and re-layouts: 3.24 us -> 0 us
  Pallas kernels: 154 us -> 152 us
    pallas_call x1, Pallas kernels: 154 us -> 150 us  [on_device(): pl.pallas_call(layer_kernel, out_shape=(jax.ShapeDtypeStruct((1, SRC, D),...]
    unnamed x2 -> x0, local copies, waits for them, and re-layouts: 3.24 us -> none
    pallas_call x0 -> x1, Pallas kernels: none -> 1.74 us  [on_device(): pl.pallas_call(leave_kernel, out_shape=(jax.ShapeDtypeStruct(memory.shape...]
where the time goes in v3:
time: 153 us
  Pallas kernels  152 us (99%)
    pallas_call x1, Pallas kernels, on_device(): pl.pallas_call(layer_kernel, out_shape=(jax.ShapeDtypeStruct((1, SRC, D),...  150 us

profile of v3, /device:TPU:0, one launch (start us, length us, event | category | flops | bytes accessed | tf_op | source)
XLA Modules:
  0.0 153.0 jit_solution(4448979274925612696)
XLA Ops:
  1.3 150.0 %shard_map.212 = (bf16[1,128,1024]{2,1,0:T(8,128)(2,1)}, bf16[1,64,1024]{2,1,0:T(8,128)(2,1)}) custom-call(bf16[1,128,1024]{2,1,0:T(8,128)(2,1)} %refs_0_.1, s32[128]{0:T(128)} %refs_1_.1, f32[1024]{0:T(1024)} %refs_2_.1, f32[4,33]{1,0:T(4,128)} %refs_3_.1, f32[1024]{0:T(1024)} %refs_4_.1, bf16[1,64,1024]{2,1,0:T(8,128)(2,1)} %refs_5_.1, s32[16]{0:T(128)} %refs_6_.1, ...), custom_call_target="tpu_custom_call" | custom-call | tf_op jit(solution)/shard_map/pallas_call | solution.py:818
  151.3 1.7 %shard_map.213 = (bf16[1,128,1024]{2,1,0:T(8,128)(2,1)}, bf16[1,64,1024]{2,1,0:T(8,128)(2,1)}) custom-call(bf16[1,128,1024]{2,1,0:T(8,128)(2,1)} %get-tuple-element.4.memory, bf16[1,64,1024]{2,1,0:T(8,128)(2,1)} %get-tuple-element.5.dec), custom_call_target="tpu_custom_call" | custom-call | tf_op jit(solution)/shard_map/pallas_call | solution.py:844

commit v4 on v3

--- a/solution.py
+++ b/solution.py
@@ -25,8 +25,9 @@
 BF16 = jnp.bfloat16
 
 GATHER_ORDER = ((0, 0), (0, 1), (0, 3), (1, 0), (0, 2), (1, 1), (1, 3), (1, 2))
-SCATTER_ORDER = ((1, 2), (1, 1), (1, 3), (0, 2), (0, 1), (0, 3), (1, 0), (0, 0))
-FFN_ORDER = ((0, 0), (0, 1), (1, 2), (0, 2), (1, 1), (1, 3), (1, 0), (0, 3))
+FFN_ORDER = ((0, 1), (1, 0), (1, 1), (1, 3), (1, 2), (0, 2))
+PAIR_DZ = 0 << 6 | 1 << 10 | 3 << 12 | 2 << 14
+PAIR_BEFORE = 0 << 10 | 1 << 12 | 3 << 14
 ROW_CHUNKS = 2
 ENC_CHUNKS = 4
 MEM_CHUNKS = 2
@@ -114,8 +115,9 @@
         p = self.p
         for target in (p.slot(0, 1), p.slot(0, 3), p.slot(1, 0), p.slot(0, 0, 1)):
             self._full(p.me, target)
-        if self.direct:
-            self._full(p.me, p.slot(0, 2))
+
+    def start_far(self):
+        self._full(self.p.me, self.p.slot(0, 2))
 
     def event(self, index):
         p = self.p
@@ -170,7 +172,7 @@
         self.yfar_sem, self.relay_sem, self.fin_sem, self.finy_sem, self.yrec_sem = sems[3:]
         self.rows = part.shape[1] // chunks
         self.half = self.rows // 2
-        self.sent = []
+        self.sent = {}
 
     @staticmethod
     def scratch(rows, chunks):
@@ -208,10 +210,9 @@
         slot = chip * 2 + self.p.core
         self.part[slot] = self.part[slot] + self.xbuf[chip]
 
-    def _send(self, src, dst, recv_sem, target):
-        sem = self.ssem.at[len(self.sent)]
-        send(src, dst, sem, recv_sem, {"tensor": target})
-        self.sent.append(src.shape[0])
+    def _send(self, key, src, dst, recv_sem, target):
+        index, _ = self.sent.setdefault(key, (len(self.sent), src.shape[0]))
+        send(src, dst, self.ssem.at[index], recv_sem, {"tensor": target})
 
     def all_rows(self, chunk):
         return pl.ds(chunk * self.rows, self.rows)
@@ -224,6 +225,7 @@
         for chunk in range(self.chunks):
             rows = self.all_rows(chunk)
             self._send(
+                ("yfar", chunk),
                 self.part.at[slot, rows],
                 self.yfar.at[rows],
                 self.yfar_sem.at[chunk],
@@ -236,6 +238,7 @@
         for chunk in range(self.chunks):
             rows = self.all_rows(chunk)
             self._send(
+                ("side", chunk, way),
                 self.part.at[slot, rows],
                 self.finy.at[way, rows],
                 self.finy_sem.at[chunk, way],
@@ -246,16 +249,31 @@
         dz = (1, 3)[way]
         rows = self.half_rows(chunk, which)
         self._send(
+            ("near", chunk, way, which),
             self.part.at[self.p.slot(0, dz), rows],
             self.fin.at[way, rows],
             self.fin_sem.at[chunk, way, which],
             self.p.slot(0, dz),
         )
 
-    def send_near(self, way):
-        for chunk in range(self.chunks):
+    def send_near(self, chunk, ways=(0, 1)):
+        for way in ways:
             for which in (0, 1):
                 self._near(chunk, way, which)
+
+    def send_role(self, chip):
+        p = self.p
+        dy, dz = (chip // 4 + p.y) % 2, (chip % 4 + 4 - p.z) % 4
+
+        def when(row, column, action):
+            @pl.when(jnp.logical_and(dy == row, dz == column))
+            def _():
+                action()
+
+        when(1, 2, self.send_yfar)
+        for way, column in ((0, 1), (1, 3)):
+            when(1, column, functools.partial(self.send_side, way))
+            when(0, column, lambda way=way: [self.send_near(c, (way,)) for c in range(self.chunks)])
 
     def far(self, chunk):
         rows = self.all_rows(chunk)
@@ -264,13 +282,18 @@
         self.part[slot, rows, :] = self.part[slot, rows, :] + self.yfar[rows, :]
         if self.direct:
             self._send(
-                self.part.at[slot, rows], self.relay.at[rows], self.relay_sem.at[chunk, 0], slot
+                ("far", chunk),
+                self.part.at[slot, rows],
+                self.relay.at[rows],
+                self.relay_sem.at[chunk, 0],
+                slot,
             )
             return
         self._near(chunk, 0, 1)
         self._near(chunk, 1, 0)
         for way in (0, 1):
             self._send(
+                ("far", chunk, way),
                 self.part.at[slot, self.half_rows(chunk, way)],
                 self.relay.at[self.half_rows(chunk, way)],
                 self.relay_sem.at[chunk, way],
@@ -288,7 +311,11 @@
     def cross_send(self, chunk):
         rows = self.all_rows(chunk)
         self._send(
-            self.ysend.at[rows], self.yrec.at[rows], self.yrec_sem.at[chunk], self.p.slot(1, 0)
+            ("cross", chunk),
+            self.ysend.at[rows],
+            self.yrec.at[rows],
+            self.yrec_sem.at[chunk],
+            self.p.slot(1, 0),
         )
 
     def relay_add(self, chunk):
@@ -336,37 +363,8 @@
         for chip in range(8):
             slot = chip * 2 + (self.p.core + 1) % 2
             arrived(self.part.at[slot], self.psem.at[chip])
-        for index, rows in enumerate(self.sent):
+        for index, rows in self.sent.values():
             arrived(self.part.at[0, pl.ds(0, rows)], self.ssem.at[index])
-
-
-def project_out(place, scatter, ctx, weight, also):
-    rows = ctx.shape[1]
-
-    def step(index, carry):
-        @pl.when(index < 8)
-        def _():
-            chip = chip_at(place, SCATTER_ORDER, index)
-            block = ctx[pl.ds(chip * 2, 2)].reshape(2 * rows, HW)
-            scatter.part[pl.ds(chip * 2, 2)] = dot(block, weight[...]).astype(BF16).reshape(2, rows, D)
-
-        @pl.when(jnp.logical_and(index > 0, index < 9))
-        def _():
-            scatter.partner_send(chip_at(place, SCATTER_ORDER, index - 1))
-
-        @pl.when(index > 1)
-        def _():
-            scatter.partner_add(chip_at(place, SCATTER_ORDER, index - 2))
-
-        for at, action in also:
-
-            @pl.when(index == at)
-            def _(action=action):
-                action()
-
-        return carry
-
-    lax.fori_loop(0, 10, step, 0)
 
 
 def dot(left, right):
@@ -390,15 +388,17 @@
         taken, refs[:count] = refs[:count], []
         return taken
 
-    tokens, lengths, gain, bias, mem_gain = take(5)
-    dec_tokens, tags, table, cross_gain, ffn_gain, tgt_length = take(6)
-    hbm = take(10)
+    small_hbm, hbm = take(11), take(10)
     memory_out, dec_out = take(2)
+    small = take(10)
+    lengths, gain, bias, mem_gain, dec_tokens = small[:5]
+    tags, table, cross_gain, ffn_gain, tgt_length = small[5:]
+    (small_sem,) = take(1)
     weights = take(10)
     (weight_sem,) = take(1)
     wq, wk, wv, wo, cq, ck, cv, co, win, wout = weights
     grid, q_s, k_s, v_s, s_s, w_s, ctx = take(7)
-    hop, hop_sem, swap_sem = take(3)
+    hop, back_sem, swap_sem = take(3)
     inp, q_all, cross_ctx, act, hidden = take(5)
     place = Place()
     enc_refs, mem_refs, dec_refs, ffn_refs = take(4), take(4), take(4), take(4)
@@ -406,7 +406,7 @@
     mem = Gather.make(place, mem_refs, MEM_CHUNKS)
     (dec,) = Gather.make(place, dec_refs, 1)
     ffn = Gather.make(place, ffn_refs, DEC_CHUNKS, True)
-    enc_sum = Scatter(place, ENC_CHUNKS, False, *take(16))
+    enc_sum = Scatter(place, ENC_CHUNKS, True, *take(16))
     cross_sum = Scatter(place, DEC_CHUNKS, True, *take(16))
     ffn_sum = Scatter(place, DEC_CHUNKS, True, *take(16))
 
@@ -419,7 +419,18 @@
         pltpu.make_async_copy(src, dst, weight_sem.at[index])
         for index, (src, dst) in enumerate(zip(hbm, weights))
     ]
-    shifted_to = place.slot(0, place.x)
+    owner = place.slot(0, 4 - place.x)
+    enc_buf, mem_buf, dec_buf, ffn_buf = enc_refs[0], mem_refs[0], dec_refs[0], ffn_refs[0]
+    fetch = [
+        pltpu.make_async_copy(src, dst, small_sem.at[index])
+        for index, (src, dst) in enumerate(zip(small_hbm[1:], small))
+    ]
+    own_rows = pltpu.make_async_copy(small_hbm[0].at[0], enc_buf.at[place.me], small_sem.at[10])
+    own_rows.start()
+    for copy in fetch:
+        copy.start()
+    for load in loads[:4]:
+        load.start()
     swap_dp = ((place.z + 4 - place.x) % 4) * 2 + place.core
     swap_t = place.y * 8 + place.z * 2 + place.y_lo
     stays = jnp.logical_and(swap_dp == place.dp, swap_t == place.me)
@@ -439,8 +450,20 @@
     def _():
         pl.semaphore_signal(barrier, inc=1, device_id=(swap_dp, swap_t), device_id_type=MESH)
 
-    enc_buf, mem_buf, dec_buf, ffn_buf = enc_refs[0], mem_refs[0], dec_refs[0], ffn_refs[0]
-    enc_buf[place.me] = rms(tokens[0].astype(F32), gain[...]).astype(BF16)
+    own_rows.wait()
+
+    @pl.when(moves)
+    def _():
+        pl.semaphore_wait(barrier, 6)
+
+    @pl.when(stays)
+    def _():
+        pl.semaphore_wait(barrier, 5)
+
+    for gather in enc:
+        gather.start()
+    for copy in fetch:
+        copy.wait()
     tag = tags[place.me]
     lang = jnp.zeros((1, D), F32)
     for index in range(LANGS):
@@ -448,19 +471,6 @@
     value = dec_tokens[0].astype(F32) + lang
     inp[...] = value
     dec_buf[place.me] = rms(value, cross_gain[...]).astype(BF16)
-    for load in loads[:4]:
-        load.start()
-
-    @pl.when(moves)
-    def _():
-        pl.semaphore_wait(barrier, 6)
-
-    @pl.when(stays)
-    def _():
-        pl.semaphore_wait(barrier, 5)
-
-    for gather in enc:
-        gather.start()
 
     keys = lax.broadcasted_iota(jnp.int32, (SRC, SRC), 1)
     bucket = jnp.clip(keys - lax.broadcasted_iota(jnp.int32, (SRC, SRC), 0), -MAXREL, MAXREL) + MAXREL
@@ -474,11 +484,14 @@
 
     items = [(ex, head) for ex in range(2) for head in range(HEADS)]
 
+    def sum_chip(index):
+        chip = chip_at(place, GATHER_ORDER, index)
+        return chip // 4 * 4 + (chip % 4 + place.x) % 4
+
     def enc_step(index, carry):
         @pl.when(index == 1)
         def _():
             events(enc, 1, 2, 3)
-            dec.start()
             for load in loads[4:]:
                 load.start()
 
@@ -486,74 +499,77 @@
         def _():
             events(enc, 4, 5, 6)
 
-        @pl.when(index == 5)
-        def _():
-            events([dec], 1, 2, 3)
-
         @pl.when(index == 7)
         def _():
             events(enc, 7)
 
-        chip = chip_at(place, GATHER_ORDER, index)
-        for gather in enc:
-            gather.partner_wait(chip)
-        rows = enc_buf[pl.ds(chip * 2, 2)].reshape(2 * SRC, D)
-        q_s[...] = dot(rows, wq[...]).astype(BF16)
-        k_s[...] = dot(rows, wk[...]).astype(BF16)
-        v_s[...] = dot(rows, wv[...]).astype(BF16)
-        columns = lax.broadcasted_iota(jnp.int32, (SRC, SRC), 1)
-        for item, (ex, head) in enumerate(items):
-            here, cols = slice(ex * SRC, (ex + 1) * SRC), slice(head * HD, (head + 1) * HD)
-            s_s[item] = dot_t(q_s[here, cols], k_s[here, cols])
-        for item, (ex, head) in enumerate(items):
-            length = lengths[place.dp * 16 + chip * 2 + ex]
-            scores = s_s[item] * SCALE + grid[head]
-            w_s[item] = softmax_weights(jnp.where(columns < length, scores, NEG_FILL))
-        for item, (ex, head) in enumerate(items):
-            here, cols = slice(ex * SRC, (ex + 1) * SRC), slice(head * HD, (head + 1) * HD)
-            ctx[chip * 2 + ex, :, cols] = dot(w_s[item], v_s[here, cols]).astype(BF16)
+        def attend():
+            chip = chip_at(place, GATHER_ORDER, index)
+            for gather in enc:
+                gather.partner_wait(chip)
+            raw = enc_buf[pl.ds(chip * 2, 2)].reshape(2 * SRC, D)
+            rows = rms(raw.astype(F32), gain[...]).astype(BF16)
+            q_s[...] = dot(rows, wq[...]).astype(BF16)
+            k_s[...] = dot(rows, wk[...]).astype(BF16)
+            v_s[...] = dot(rows, wv[...]).astype(BF16)
+            columns = lax.broadcasted_iota(jnp.int32, (SRC, SRC), 1)
+            for item, (ex, head) in enumerate(items):
+                here, cols = slice(ex * SRC, (ex + 1) * SRC), slice(head * HD, (head + 1) * HD)
+                s_s[item] = dot_t(q_s[here, cols], k_s[here, cols])
+            for item, (ex, head) in enumerate(items):
+                length = lengths[place.dp * 16 + chip * 2 + ex]
+                scores = s_s[item] * SCALE + grid[head]
+                w_s[item] = softmax_weights(jnp.where(columns < length, scores, NEG_FILL))
+            for item, (ex, head) in enumerate(items):
+                here, cols = slice(ex * SRC, (ex + 1) * SRC), slice(head * HD, (head + 1) * HD)
+                ctx[here, cols] = dot(w_s[item], v_s[here, cols]).astype(BF16)
+
+        attend()
+
+        @pl.when(index > 1)
+        def _():
+            done = sum_chip(index - 2)
+            enc_sum.partner_add(done)
+            enc_sum.send_role(done)
+
+        terms = dot(ctx[...], wo[...]).astype(BF16).reshape(2, SRC, D)
+        enc_sum.part[pl.ds(sum_chip(index) * 2, 2)] = terms
+
+        @pl.when(index > 0)
+        def _():
+            enc_sum.partner_send(sum_chip(index - 1))
+
         return carry
 
     lax.fori_loop(0, 8, enc_step, 0)
-
-    project_out(
-        place,
-        enc_sum,
-        ctx,
-        wo,
-        (
-            (1, functools.partial(events, [dec], 4, 5, 6, 7)),
-            (3, enc_sum.send_yfar),
-            (4, functools.partial(enc_sum.send_side, 0)),
-            (5, functools.partial(enc_sum.send_side, 1)),
-        ),
-    )
+    enc_sum.partner_send(sum_chip(7))
+    for index in (6, 7):
+        done = sum_chip(index)
+        enc_sum.partner_add(done)
+        enc_sum.send_role(done)
+    for chunk in range(ENC_CHUNKS):
+        enc_sum.far(chunk)
+    dec.start()
 
     def finish_memory(chunk):
         rows = enc_sum.all_rows(chunk)
-        value = tokens[0, rows, :].astype(F32) + enc_sum.total(chunk)
-        memory_out[0, rows, :] = rms(value, mem_gain[...]).astype(BF16)
-
-    def shift_send(chunk):
-        rows = enc_sum.all_rows(chunk)
-
+        value = enc_buf[owner, rows, :].astype(F32) + enc_sum.total(chunk)
+        hop[rows, :] = rms(value, mem_gain[...]).astype(BF16)
+
+    def give_back():
         @pl.when(place.x == 0)
         def _():
-            pltpu.make_async_copy(memory_out.at[0, rows], hop.at[rows], hop_sem.at[1, chunk]).start()
+            pltpu.make_async_copy(hop, memory_out.at[0], back_sem.at[1]).start()
 
         @pl.when(place.x > 0)
         def _():
-            send(
-                memory_out.at[0, rows],
-                hop.at[rows],
-                hop_sem.at[0, chunk],
-                hop_sem.at[1, chunk],
-                {"tensor": shifted_to},
-            )
+            send(hop, memory_out.at[0], back_sem.at[0], back_sem.at[1], {"tensor": owner})
 
     def swap_send(chunk):
         rows = enc_sum.all_rows(chunk)
-        arrived(hop.at[rows], hop_sem.at[1, chunk])
+
+        if chunk == ENC_CHUNKS - 1:
+            events([dec], 1, 2, 3)
 
         @pl.when(stays)
         def _():
@@ -578,7 +594,8 @@
         if chunk % each == each - 1:
             mem[chunk // each].start()
 
-    enc_sum.run(finish_memory, shift_send, swap_send, spread)
+    enc_sum.run(finish_memory, swap_send, spread)
+    events([dec], 4, 5, 6, 7)
 
     for chip in range(8):
         dec.partner_wait(chip)
@@ -591,6 +608,14 @@
         return carry
 
     lax.fori_loop(0, 4, q_step, 0)
+
+    def cross_chip(dz):
+        return (place.z + dz + 4 - place.x) % 4 * 2
+
+    def sum_cross(dz):
+        for chip in (cross_chip(dz), cross_chip(dz) + 1):
+            cross_sum.partner_add(chip)
+            cross_sum.send_role(chip)
 
     def cross_step(index, carry):
         @pl.when(index == 1)
@@ -624,23 +649,25 @@
         for item, (ex, head) in enumerate(items):
             here, cols = slice(ex * SRC, (ex + 1) * SRC), slice(head * HD, (head + 1) * HD)
             cross_ctx[base + 2 * ex, :, cols] = dot(w_s[item, :TGT, :], v_s[here, cols]).astype(BF16)
+
+        @pl.when(jnp.logical_or(index == 3, index > 4))
+        def _():
+            @pl.when(index > 3)
+            def _():
+                sum_cross((PAIR_BEFORE >> (2 * index)) & 3)
+
+            first = cross_chip((PAIR_DZ >> (2 * index)) & 3)
+            block = cross_ctx[pl.ds(first * 2, 4)].reshape(4 * TGT, HW)
+            cross_sum.part[pl.ds(first * 2, 4)] = dot(block, co[...]).astype(BF16).reshape(4, TGT, D)
+            cross_sum.partner_send(first)
+            cross_sum.partner_send(first + 1)
+
         return carry
 
     lax.fori_loop(0, 8, cross_step, 0)
-    project_out(
-        place,
-        cross_sum,
-        cross_ctx,
-        co,
-        (
-            (3, cross_sum.send_yfar),
-            (4, functools.partial(cross_sum.send_side, 0)),
-            (5, functools.partial(cross_sum.send_side, 1)),
-            (7, functools.partial(cross_sum.send_near, 0)),
-            (8, functools.partial(cross_sum.send_near, 1)),
-            (9, lambda: [cross_sum.far(chunk) for chunk in range(DEC_CHUNKS)]),
-        ),
-    )
+    sum_cross(2)
+    for chunk in range(DEC_CHUNKS):
+        cross_sum.far(chunk)
 
     def finish_hidden(chunk):
         rows = cross_sum.all_rows(chunk)
@@ -649,77 +676,94 @@
         ffn_buf[place.me, rows, :] = rms(value, ffn_gain[...]).astype(BF16)
 
     cross_sum.run(finish_hidden, lambda chunk: ffn[chunk].start())
+    for gather in ffn:
+        gather.start_far()
     for load in loads[8:]:
         load.wait()
 
+    def ffn_chips(chips):
+        rows = [ffn_buf[pl.ds(chip * 2, 2)].reshape(2 * TGT, D) for chip in chips]
+        rows = rows[0] if len(chips) == 1 else jnp.concatenate(rows, axis=0)
+        count = rows.shape[0]
+        for tile in range(FF // 512):
+            cols = slice(tile * 512, (tile + 1) * 512)
+            act[:count, cols] = jnp.maximum(dot(rows, win[:, cols]), 0.0).astype(BF16)
+        yield
+        for tile in range(D // 256):
+            cols = slice(tile * 256, (tile + 1) * 256)
+            result = dot(act[:count, :], wout[:, cols]).astype(BF16)
+            for index, chip in enumerate(chips):
+                here = slice(index * 2 * TGT, (index + 1) * 2 * TGT)
+                ffn_sum.part[pl.ds(chip * 2, 2), :, cols] = result[here].reshape(2, TGT, 256)
+        for chip in chips:
+            ffn_sum.partner_send(chip)
+
+    def ready(*chips):
+        for chip in chips:
+            for gather in ffn:
+                gather.partner_wait(chip)
+
+    own = place.chip(0, 0)
+    ready(own)
+    for _ in ffn_chips([own]):
+        pass
+
     def ffn_step(index, carry):
         @pl.when(index == 0)
         def _():
-            events(ffn, 1, 2, 3, 4)
+            events(ffn, 1, 2, 3)
 
         @pl.when(index == 1)
         def _():
-            events(ffn, 5, 6, 7)
-
-        first = chip_at(place, FFN_ORDER, index * 2)
-        second = chip_at(place, FFN_ORDER, index * 2 + 1)
+            events(ffn, 4, 5, 6)
+
+        @pl.when(index == 2)
+        def _():
+            events(ffn, 7)
+            ready(place.chip(0, 3))
+
+        chips = [chip_at(place, FFN_ORDER, index * 2 + item) for item in range(2)]
+        ready(*chips)
+        halfway = ffn_chips(chips)
+        next(halfway)
 
         @pl.when(index == 0)
         def _():
-            for chip in range(2):
-                for gather in ffn:
-                    gather.partner_wait(place.chip(*FFN_ORDER[chip]))
+            ffn_sum.partner_add(own)
+
+        @pl.when(index > 0)
+        def _():
+            for item in range(2):
+                ffn_sum.partner_add(chip_at(place, FFN_ORDER, index * 2 - 2 + item))
 
         @pl.when(index == 1)
         def _():
-            for chip in range(2, 8):
-                for gather in ffn:
-                    gather.partner_wait(place.chip(*FFN_ORDER[chip]))
-
-        rows = jnp.concatenate(
-            [
-                ffn_buf[pl.ds(first * 2, 2)].reshape(2 * TGT, D),
-                ffn_buf[pl.ds(second * 2, 2)].reshape(2 * TGT, D),
-            ],
-            axis=0,
-        )
-        for tile in range(FF // 512):
-            cols = slice(tile * 512, (tile + 1) * 512)
-            act[:, cols] = jnp.maximum(dot(rows, win[:, cols]), 0.0).astype(BF16)
-
-        @pl.when(index > 0)
-        def _():
-            ffn_sum.partner_add(chip_at(place, FFN_ORDER, index * 2 - 2))
-            ffn_sum.partner_add(chip_at(place, FFN_ORDER, index * 2 - 1))
-
-        @pl.when(index == 1)
-        def _():
-            ffn_sum.send_near(0)
+            for chunk in range(DEC_CHUNKS):
+                ffn_sum.send_near(chunk, (0,))
 
         @pl.when(index == 2)
-        def _():
-            ffn_sum.send_yfar()
-
-        @pl.when(index == 3)
         def _():
             ffn_sum.send_side(0)
             ffn_sum.send_side(1)
-            for chunk in range(DEC_CHUNKS):
-                ffn_sum.far(chunk)
-
-        for tile in range(D // 256):
-            cols = slice(tile * 256, (tile + 1) * 256)
-            result = dot(act[...], wout[:, cols]).astype(BF16)
-            ffn_sum.part[pl.ds(first * 2, 2), :, cols] = result[: 2 * TGT].reshape(2, TGT, 256)
-            ffn_sum.part[pl.ds(second * 2, 2), :, cols] = result[2 * TGT :].reshape(2, TGT, 256)
-        ffn_sum.partner_send(first)
-        ffn_sum.partner_send(second)
+
+        for _ in halfway:
+            pass
         return carry
 
-    lax.fori_loop(0, 4, ffn_step, 0)
-    for index in (6, 7):
-        ffn_sum.partner_add(place.chip(*FFN_ORDER[index]))
-    ffn_sum.send_near(1)
+    lax.fori_loop(0, 3, ffn_step, 0)
+    last = ffn_chips([place.chip(0, 3)])
+    next(last)
+    for item in (4, 5):
+        ffn_sum.partner_add(place.chip(*FFN_ORDER[item]))
+    ffn_sum.send_yfar()
+    for _ in last:
+        pass
+    for chunk in range(DEC_CHUNKS):
+        ffn_sum.far(chunk)
+    ffn_sum.partner_add(place.chip(0, 3))
+    for chunk in range(DEC_CHUNKS):
+        ffn_sum.send_near(chunk, (1,))
+    give_back()
 
     def finish_out(chunk):
         rows = ffn_sum.all_rows(chunk)
@@ -729,16 +773,16 @@
 
     ffn_sum.run(finish_out)
 
-    for chunk in range(ENC_CHUNKS):
-        rows = enc_sum.all_rows(chunk)
-
-        @pl.when(place.x > 0)
-        def _(rows=rows, chunk=chunk):
-            arrived(hop.at[rows], hop_sem.at[0, chunk])
-
-        @pl.when(moves)
-        def _(rows=rows, chunk=chunk):
-            arrived(hop.at[rows], swap_sem.at[0, chunk])
+    arrived(memory_out.at[0], back_sem.at[1])
+
+    @pl.when(place.x > 0)
+    def _():
+        arrived(hop, back_sem.at[0])
+
+    @pl.when(moves)
+    def _():
+        for chunk in range(ENC_CHUNKS):
+            arrived(hop.at[enc_sum.all_rows(chunk)], swap_sem.at[0, chunk])
 
     for stage in [*enc, dec, *mem, *ffn, enc_sum, cross_sum, ffn_sum]:
         stage.drain()
@@ -788,8 +832,23 @@
         ffn_in,
         ffn_out,
     ]
-    spaces = [VM, SM, VM, SM, VM, VM, SM, VM, VM, VM, SM] + [pl.ANY] * len(weights)
-    scratch = [pltpu.VMEM(weight.shape, BF16) for weight in weights]
+    small = [
+        enc_tokens,
+        src_lengths,
+        enc_gain,
+        enc_bias,
+        mem_gain,
+        dec_tokens,
+        lang_tags,
+        lang_table,
+        cross_gain,
+        ffn_gain,
+        tgt_lengths,
+    ]
+    spaces = [SM, VM, SM, VM, VM, SM, VM, VM, VM, SM]
+    scratch = [space(value.shape, value.dtype) for space, value in zip(spaces, small[1:])]
+    scratch += [pltpu.SemaphoreType.DMA((len(small),))]
+    scratch += [pltpu.VMEM(weight.shape, BF16) for weight in weights]
     scratch += [
         pltpu.SemaphoreType.DMA((len(weights),)),
         pltpu.VMEM((HEADS, SRC, SRC), F32),
@@ -798,9 +857,9 @@
         pltpu.VMEM((2 * SRC, HW), BF16),
         pltpu.VMEM((2 * HEADS, SRC, SRC), F32),
         pltpu.VMEM((2 * HEADS, SRC, SRC), BF16),
-        pltpu.VMEM((16, SRC, HW), BF16),
+        pltpu.VMEM((2 * SRC, HW), BF16),
         pltpu.VMEM((SRC, D), BF16),
-        pltpu.SemaphoreType.DMA((2, ENC_CHUNKS)),
+        pltpu.SemaphoreType.DMA((2,)),
         pltpu.SemaphoreType.DMA((2, ENC_CHUNKS)),
         pltpu.VMEM((TGT, D), F32),
         pltpu.VMEM((16, TGT, HW), BF16),
@@ -821,26 +880,13 @@
             jax.ShapeDtypeStruct((1, SRC, D), BF16),
             jax.ShapeDtypeStruct((1, TGT, D), BF16),
         ),
-        in_specs=[pl.BlockSpec(memory_space=space) for space in spaces],
+        in_specs=[pl.BlockSpec(memory_space=pl.ANY)] * (len(small) + len(weights)),
         out_specs=(pl.BlockSpec(memory_space=VM), pl.BlockSpec(memory_space=VM)),
         scratch_shapes=scratch,
         compiler_params=pltpu.CompilerParams(
             collective_id=1, has_side_effects=True, vmem_limit_bytes=67_043_328
         ),
-    )(
-        enc_tokens,
-        src_lengths,
-        enc_gain,
-        enc_bias,
-        mem_gain,
-        dec_tokens,
-        lang_tags,
-        lang_table,
-        cross_gain,
-        ffn_gain,
-        tgt_lengths,
-        *weights,
-    )
+    )(*small, *weights)
     return pl.pallas_call(
         leave_kernel,
         out_shape=(

time: 153 us -> 155 us (1.013)
  the two profiles are of different devices: /device:TPU:0 before, /device:TPU:7 now
where the time goes in v4:
time: 155 us; the launch traced here: 154 us
  Pallas kernels  153 us (99%)
    pallas_call x1, Pallas kernels, on_device(): pl.pallas_call(layer_kernel, out_shape=(jax.ShapeDtypeStruct((1, SRC, D),...  151 us

profile of v4, /device:TPU:7, one launch (start us, length us, event | category | flops | bytes accessed | tf_op | source)
XLA Modules:
  0.0 154.4 jit_solution(10772543634187034905)
XLA Ops:
  1.3 151.4 %shard_map.212 = (bf16[1,128,1024]{2,1,0:T(8,128)(2,1)}, bf16[1,64,1024]{2,1,0:T(8,128)(2,1)}) custom-call(bf16[1,128,1024]{2,1,0:T(8,128)(2,1)} %refs_0_.1, s32[128]{0:T(128)} %refs_1_.1, f32[1024]{0:T(1024)} %refs_2_.1, f32[4,33]{1,0:T(4,128)} %refs_3_.1, f32[1024]{0:T(1024)} %refs_4_.1, bf16[1,64,1024]{2,1,0:T(8,128)(2,1)} %refs_5_.1, s32[16]{0:T(128)} %refs_6_.1, ...), custom_call_target="tpu_custom_call" | custom-call | tf_op jit(solution)/shard_map/pallas_call | solution.py:877
  152.7 1.7 %shard_map.213 = (bf16[1,128,1024]{2,1,0:T(8,128)(2,1)}, bf16[1,64,1024]{2,1,0:T(8,128)(2,1)}) custom-call(bf16[1,128,1024]{2,1,0:T(8,128)(2,1)} %get-tuple-element.4.memory, bf16[1,64,1024]{2,1,0:T(8,128)(2,1)} %get-tuple-element.5.dec), custom_call_target="tpu_custom_call" | custom-call | tf_op jit(solution)/shard_map/pallas_call | solution.py:890

commit v5 on v4

--- a/solution.py
+++ b/solution.py
@@ -404,15 +404,15 @@
     enc_refs, mem_refs, dec_refs, ffn_refs = take(4), take(4), take(4), take(4)
     enc = Gather.make(place, enc_refs, ROW_CHUNKS)
     mem = Gather.make(place, mem_refs, MEM_CHUNKS)
-    (dec,) = Gather.make(place, dec_refs, 1)
+    (dec,) = Gather.make(place, dec_refs, 1, True)
     ffn = Gather.make(place, ffn_refs, DEC_CHUNKS, True)
     enc_sum = Scatter(place, ENC_CHUNKS, True, *take(16))
     cross_sum = Scatter(place, DEC_CHUNKS, True, *take(16))
     ffn_sum = Scatter(place, DEC_CHUNKS, True, *take(16))
 
     def events(gathers, *numbers):
-        for gather in gathers:
-            for number in numbers:
+        for number in numbers:
+            for gather in gathers:
                 gather.event(number)
 
     loads = [
@@ -549,6 +549,7 @@
         enc_sum.send_role(done)
     for chunk in range(ENC_CHUNKS):
         enc_sum.far(chunk)
+    dec.start_far()
     dec.start()
 
     def finish_memory(chunk):
@@ -568,8 +569,8 @@
     def swap_send(chunk):
         rows = enc_sum.all_rows(chunk)
 
-        if chunk == ENC_CHUNKS - 1:
-            events([dec], 1, 2, 3)
+        if chunk == ENC_CHUNKS - 2:
+            events([dec], 4, 1, 2, 3)
 
         @pl.when(stays)
         def _():
@@ -589,13 +590,14 @@
 
     def spread(chunk):
         rows = enc_sum.all_rows(chunk)
+        if chunk == ENC_CHUNKS - 1:
+            events([dec], 5, 6, 7)
         arrived(mem_buf.at[place.me, rows], swap_sem.at[1, chunk])
         each = ENC_CHUNKS // MEM_CHUNKS
         if chunk % each == each - 1:
             mem[chunk // each].start()
 
     enc_sum.run(finish_memory, swap_send, spread)
-    events([dec], 4, 5, 6, 7)
 
     for chip in range(8):
         dec.partner_wait(chip)
@@ -716,6 +718,7 @@
         @pl.when(index == 1)
         def _():
             events(ffn, 4, 5, 6)
+            give_back()
 
         @pl.when(index == 2)
         def _():
@@ -763,7 +766,6 @@
     ffn_sum.partner_add(place.chip(0, 3))
     for chunk in range(DEC_CHUNKS):
         ffn_sum.send_near(chunk, (1,))
-    give_back()
 
     def finish_out(chunk):
         rows = ffn_sum.all_rows(chunk)

time: 155 us -> 145 us (0.935)
  the two profiles are of different devices: /device:TPU:7 before, /device:TPU:0 now
where the time goes in v5:
time: 145 us
  Pallas kernels  143 us (99%)
    pallas_call x1, Pallas kernels, on_device(): pl.pallas_call(layer_kernel, out_shape=(jax.ShapeDtypeStruct((1, SRC, D),...  142 us

profile of v5, /device:TPU:0, one launch (start us, length us, event | category | flops | bytes accessed | tf_op | source)
XLA Modules:
  0.0 144.6 jit_solution(981079026021317549)
XLA Ops:
  1.3 141.6 %shard_map.212 = (bf16[1,128,1024]{2,1,0:T(8,128)(2,1)}, bf16[1,64,1024]{2,1,0:T(8,128)(2,1)}) custom-call(bf16[1,128,1024]{2,1,0:T(8,128)(2,1)} %refs_0_.1, s32[128]{0:T(128)} %refs_1_.1, f32[1024]{0:T(1024)} %refs_2_.1, f32[4,33]{1,0:T(4,128)} %refs_3_.1, f32[1024]{0:T(1024)} %refs_4_.1, bf16[1,64,1024]{2,1,0:T(8,128)(2,1)} %refs_5_.1, s32[16]{0:T(128)} %refs_6_.1, ...), custom_call_target="tpu_custom_call" | custom-call | tf_op jit(solution)/shard_map/pallas_call | solution.py:879
  142.9 1.7 %shard_map.213 = (bf16[1,128,1024]{2,1,0:T(8,128)(2,1)}, bf16[1,64,1024]{2,1,0:T(8,128)(2,1)}) custom-call(bf16[1,128,1024]{2,1,0:T(8,128)(2,1)} %get-tuple-element.4.memory, bf16[1,64,1024]{2,1,0:T(8,128)(2,1)} %get-tuple-element.5.dec), custom_call_target="tpu_custom_call" | custom-call | tf_op jit(solution)/shard_map/pallas_call | solution.py:892

commit v6 on v5

--- a/solution.py
+++ b/solution.py
@@ -28,10 +28,10 @@
 FFN_ORDER = ((0, 1), (1, 0), (1, 1), (1, 3), (1, 2), (0, 2))
 PAIR_DZ = 0 << 6 | 1 << 10 | 3 << 12 | 2 << 14
 PAIR_BEFORE = 0 << 10 | 1 << 12 | 3 << 14
-ROW_CHUNKS = 2
+ROW_CHUNKS = 1
 ENC_CHUNKS = 4
 MEM_CHUNKS = 2
-DEC_CHUNKS = 2
+DEC_CHUNKS = 1
 
 
 def packed(order):

time: 145 us -> 144 us (level)
  no operation moved by 1% of the time
where the time goes in v6:
time: 144 us; the launch traced here: 143 us
  Pallas kernels  142 us (99%)
    pallas_call x1, Pallas kernels, on_device(): pl.pallas_call(layer_kernel, out_shape=(jax.ShapeDtypeStruct((1, SRC, D),...  140 us

profile of v6, /device:TPU:0, one launch (start us, length us, event | category | flops | bytes accessed | tf_op | source)
XLA Modules:
  0.0 143.3 jit_solution(3203105442971574495)
XLA Ops:
  1.3 140.3 %shard_map.212 = (bf16[1,128,1024]{2,1,0:T(8,128)(2,1)}, bf16[1,64,1024]{2,1,0:T(8,128)(2,1)}) custom-call(bf16[1,128,1024]{2,1,0:T(8,128)(2,1)} %refs_0_.1, s32[128]{0:T(128)} %refs_1_.1, f32[1024]{0:T(1024)} %refs_2_.1, f32[4,33]{1,0:T(4,128)} %refs_3_.1, f32[1024]{0:T(1024)} %refs_4_.1, bf16[1,64,1024]{2,1,0:T(8,128)(2,1)} %refs_5_.1, s32[16]{0:T(128)} %refs_6_.1, ...), custom_call_target="tpu_custom_call" | custom-call | tf_op jit(solution)/shard_map/pallas_call | solution.py:879
  141.6 1.7 %shard_map.213 = (bf16[1,128,1024]{2,1,0:T(8,128)(2,1)}, bf16[1,64,1024]{2,1,0:T(8,128)(2,1)}) custom-call(bf16[1,128,1024]{2,1,0:T(8,128)(2,1)} %get-tuple-element.4.memory, bf16[1,64,1024]{2,1,0:T(8,128)(2,1)} %get-tuple-element.5.dec), custom_call_target="tpu_custom_call" | custom-call | tf_op jit(solution)/shard_map/pallas_call | solution.py:892

commit v7 on v6

--- a/solution.py
+++ b/solution.py
@@ -714,11 +714,11 @@
         @pl.when(index == 0)
         def _():
             events(ffn, 1, 2, 3)
+            give_back()
 
         @pl.when(index == 1)
         def _():
             events(ffn, 4, 5, 6)
-            give_back()
 
         @pl.when(index == 2)
         def _():

time: 144 us -> 145 us (level)
  no operation moved by 1% of the time
where the time goes in v7:
time: 145 us; the launch traced here: 143 us
  Pallas kernels  142 us (98%)
    pallas_call x1, Pallas kernels, on_device(): pl.pallas_call(layer_kernel, out_shape=(jax.ShapeDtypeStruct((1, SRC, D),...  140 us

profile of v7, /device:TPU:0, one launch (start us, length us, event | category | flops | bytes accessed | tf_op | source)
XLA Modules:
  0.0 143.3 jit_solution(17226224552326142355)
XLA Ops:
  1.3 140.3 %shard_map.212 = (bf16[1,128,1024]{2,1,0:T(8,128)(2,1)}, bf16[1,64,1024]{2,1,0:T(8,128)(2,1)}) custom-call(bf16[1,128,1024]{2,1,0:T(8,128)(2,1)} %refs_0_.1, s32[128]{0:T(128)} %refs_1_.1, f32[1024]{0:T(1024)} %refs_2_.1, f32[4,33]{1,0:T(4,128)} %refs_3_.1, f32[1024]{0:T(1024)} %refs_4_.1, bf16[1,64,1024]{2,1,0:T(8,128)(2,1)} %refs_5_.1, s32[16]{0:T(128)} %refs_6_.1, ...), custom_call_target="tpu_custom_call" | custom-call | tf_op jit(solution)/shard_map/pallas_call | solution.py:879
  141.6 1.7 %shard_map.213 = (bf16[1,128,1024]{2,1,0:T(8,128)(2,1)}, bf16[1,64,1024]{2,1,0:T(8,128)(2,1)}) custom-call(bf16[1,128,1024]{2,1,0:T(8,128)(2,1)} %get-tuple-element.4.memory, bf16[1,64,1024]{2,1,0:T(8,128)(2,1)} %get-tuple-element.5.dec), custom_call_target="tpu_custom_call" | custom-call | tf_op jit(solution)/shard_map/pallas_call | solution.py:892
